TPU v7x, 256 devices: a whole 4x4x8 slice. The times are simulated.
256 devices in a mesh: tok: 32 (over z_lo, y, core), col: 8 (over x, z_hi).
Axes of the slice: x: 4, y: 4, z: 8 (z_hi: 2, z_lo: 4; z = z_hi * 4 + z_lo), core: 2. Of those that a mesh axis runs over, the one named last changes fastest.
Arguments:
- hidden: bfloat16 [8192, 8192], P('tok'), may hold values from -6 to 6
- norm_gain: float32 [8192], replicated, may hold values from 0.1 to 1.9
- token_ids: int32 [8192], P('tok'), may hold values from 0 to 128000, as said below
- owner: int32 [1], replicated, may hold values from 0 to 31
- query_store: bfloat16 [32, 8192, 4096], P('tok', None, 'col'), may hold values from -0.0625 to 0.0625
- key_store: bfloat16 [32, 8192, 512], P('tok', None, 'col'), may hold values from -0.0625 to 0.0625
Outputs:
- queries: bfloat16 [8192, 4096], P('tok', 'col')
- keys: bfloat16 [8192, 512], P('tok', 'col')
- hessian: float32 [8192, 8192], P('col', 'tok')
Inputs may be any that keep to these rules, and one draw needn't show every extreme that they name: `token_ids`: id 128000 marks the first token of a document; every other id is below it.
All inputs are finite; a program needn't handle non-finite values.
Results may differ from a plain program's by a relative error of at most 0.0049.
Values may be sent and summed in bfloat16 or wider, within the bound.
No kernel may reach another device: no remote copies, remote signals or barrier semaphores. Data moves between devices by JAX's collectives and lax.ppermute only.
A program may use at most 128 MiB of HBM per device.

v0:
```python
import jax
import jax.numpy as jnp
from jax import lax
from jax.sharding import PartitionSpec as P

HEAD = 128
SEQ = 128


begin_token = 128000
rope_base = 500000.0


def spread(array, axis, root):
    mine = lax.axis_index(axis) == root
    return lax.psum(jnp.where(mine, array, jnp.zeros_like(array)), axis)


def positions(token_ids):
    samples = token_ids.reshape(-1, SEQ)
    index = jnp.arange(SEQ, dtype=jnp.int32)
    starts = jnp.where(samples == begin_token, index[None, :], jnp.zeros_like(samples))
    latest = lax.cummax(starts, axis=1)
    return (index[None, :] - latest).reshape(-1)


def rotate(values, place, start):
    width = values.shape[1]
    dims = (start + jnp.arange(width, dtype=jnp.int32)) % HEAD
    pair = (dims[0::2] // 2).astype(jnp.float32)
    freq = jnp.power(jnp.float32(rope_base), -2.0 * pair / HEAD)
    angle = place.astype(jnp.float32)[:, None] * freq[None, :]
    cosine = jnp.cos(angle)
    sine = jnp.sin(angle)
    even = values[:, 0::2]
    odd = values[:, 1::2]
    first = even * cosine - odd * sine
    second = even * sine + odd * cosine
    return jnp.stack([first, second], axis=-1).reshape(values.shape[0], width)


def normalize(hidden, norm_gain):
    wide = hidden.astype(jnp.float32)
    meansq = jnp.mean(wide * wide, axis=-1, keepdims=True)
    return (wide * lax.rsqrt(meansq + 1e-05) * norm_gain[None, :]).astype(jnp.bfloat16)


def transposed_product(left, right):
    return lax.dot_general(
        left, right, (((0,), (0,)), ((), ())), preferred_element_type=jnp.float32
    )


def shards(hidden, norm_gain, token_ids, owner, query_store, key_store):
    normed = normalize(hidden, norm_gain)
    place = positions(token_ids)
    column = lax.axis_index("col")
    row_width = normed.shape[1] // lax.axis_size("col")
    row_block = lax.dynamic_slice_in_dim(normed, column * row_width, row_width, 1)
    total_tokens = normed.shape[0] * lax.axis_size("tok")
    weight_q, weight_k = (
        spread(query_store[0], "tok", owner[0]),
        spread(key_store[0], "tok", owner[0]),
    )
    col_block = lax.all_to_all(normed, "tok", split_axis=1, concat_axis=0, tiled=True)
    gathered = lax.all_gather(row_block, "tok", axis=0, tiled=True)
    gram = transposed_product(gathered, col_block)
    hessian = gram * (2.0 / total_tokens)
    raw_q = jnp.dot(normed, weight_q, preferred_element_type=jnp.float32)
    raw_k = jnp.dot(normed, weight_k, preferred_element_type=jnp.float32)
    queries = rotate(raw_q, place, column * weight_q.shape[1]).astype(jnp.bfloat16)
    keys = rotate(raw_k, place, column * weight_k.shape[1]).astype(jnp.bfloat16)
    return (queries, keys, hessian)


def solution(mesh):
    placed = (P("tok", None), P(), P("tok"), P(), P("tok", None, "col"), P("tok", None, "col"))
    return jax.shard_map(
        shards,
        mesh=mesh,
        in_specs=placed,
        out_specs=(P("tok", "col"), P("tok", "col"), P("col", "tok")),
        check_vma=False,
    )
```

profile of v0, /device:TPU:132, one launch (start us, length us, event | category | flops | bytes accessed | tf_op | source)
XLA Modules:
  0.0 498.4 jit_solution(13935779070993136472)
XLA Ops:
  7.2 0.0 all-reduce.3.cloned.1.call-start
  7.9 0.0 copy-start.1
  7.9 3.8 select_bitcast_fusion
  11.6 0.0 copy-done.1
  11.7 1.0 select_bitcast_fusion.1
  12.7 0.0 all-reduce.3.cloned.1.call-update
  12.7 0.0 copy-start.2
  12.7 0.0 all-gather.2.cloned.1.call-start
  12.8 6.4 %copy.12 = bf16[256,8192]{0,1:T(8,128)(2,1)} copy(bf16[256,8192]{1,0:T(8,128)(2,1)} %param.6) | data formatting | bytes 8388608 | tf_op args[0]
  19.1 3.3 fusion
  22.5 0.0 copy-done.2
  22.5 0.0 copy-start.3
  22.5 2.9 fusion.2
  25.3 0.0 copy-start
  25.3 2.0 copy-done
  27.4 0.9 constant_dynamic-slice_fusion
  28.3 0.0 all-gather.2.cloned.1.call-update
  28.3 8.6 %all-to-all-start = ((bf16[256,32,256]{0,2,1:T(8,128)(2,1)}), bf16[256,32,256]{0,2,1:T(8,128)(2,1)}, u32[]{:S(2)}, u32[]{:S(2)}) async-start(bf16[256,32,256]{0,2,1:T(8,128)(2,1)} %bitcast.31), calls=%async_computation | async-start | bytes 8388608 | tf_op jit(solution)/shard_map/all_to_all | solution.py:65
  37.0 0.1 slice.22
  37.1 0.2 slice.19
  37.3 0.0 copy-done.3
  37.3 0.3 reduce_window_max.10
  37.7 114.6 %all-to-all-done = bf16[256,32,256]{0,2,1:T(8,128)(2,1)} async-done(((bf16[256,32,256]{0,2,1:T(8,128)(2,1)}), bf16[256,32,256]{0,2,1:T(8,128)(2,1)}, u32[]{:S(2)}, u32[]{:S(2)}) %all-to-all-start) | async-done | bytes 4194336 | tf_op jit(solution)/shard_map/all_to_all | solution.py:65
  152.3 6.4 %copy.15 = bf16[32,256,256]{2,1,0:T(8,128)(2,1)} copy(bf16[32,256,256]{1,2,0:T(8,128)(2,1)} %bitcast.10) | data formatting | bytes 8388608 | tf_op jit(solution)/shard_map/all_to_all | solution.py:65
  158.8 197.7 %all-reduce.3.cloned.1.call-done = (bf16[8192,512]{1,0:T(8,128)(2,1)}, bf16[8192,64]{0,1:T(8,128)(2,1)}) async-done(((bf16[8192,512]{1,0:T(8,128)(2,1)}, bf16[8192,64]{0,1:T(8,128)(2,1)}), (bf16[8192,512]{1,0:T(8,128)(2,1)}, bf16[8192,64]{0,1:T(8,128)(2,1)})) %all-reduce.3.cloned.1.call-update) | async-done | bytes 9437200 | tf_op jit(solution)/shard_map/psum | solution.py:16
  356.4 3.3 fusion.26
  359.8 7.0 %fusion.25 = f32[256,512]{1,0:T(8,128)S(1)} fusion(bf16[256,8192]{0,1:T(8,128)(2,1)} %copy-done, bf16[8192,512]{1,0:T(8,128)(2,1)} %get-tuple-element.9), kind=kOutput, calls=%fused_computation.56 | convolution fusion | flops 2147483648 | bytes 13107200 | tf_op jit(solution)/shard_map/dot_general | solution.py:69
  366.8 11.7 %slice.18 = f32[256,256]{1,0:T(8,128)S(1)} slice(f32[256,512]{1,0:T(8,128)S(1)} %fusion.25), slice={[0:256:1], [0:512:2]} | slice | bytes 524288 | tf_op jit(solution)/shard_map/slice | solution.py:35
  378.5 11.7 %slice.20 = f32[256,256]{1,0:T(8,128)S(1)} slice(f32[256,512]{1,0:T(8,128)S(1)} %fusion.25), slice={[0:256:1], [1:512:2]} | slice | bytes 524288 | tf_op jit(solution)/shard_map/slice | solution.py:36
  390.2 0.2 fusion.22
  390.4 0.6 convert_element_type.38
  391.1 1.4 fusion.12
  392.5 0.2 copy.13
  392.7 0.1 convert_element_type.36
  392.8 0.8 copy.16
  393.6 85.5 %all-gather.2.cloned.1.call-done = bf16[8192,1024]{0,1:T(8,128)(2,1)} async-done(((bf16[256,1024]{0,1:T(8,128)(2,1)}), bf16[8192,1024]{0,1:T(8,128)(2,1)}) %all-gather.2.cloned.1.call-update) | async-done | bytes 16777232 | tf_op jit(solution)/shard_map/all_gather | solution.py:66
  479.1 12.4 %convolution_multiply_fusion = f32[1024,256]{1,0:T(8,128)} fusion(bf16[8192,1024]{0,1:T(8,128)(2,1)} %all-gather.2.cloned.1.call-done, bf16[8192,256]{1,0:T(8,128)(2,1)} %bitcast.32), kind=kOutput, calls=%fused_computation.6 | convolution fusion | flops 4295229440 | bytes 22020096 | tf_op jit(solution)/shard_map/dot_general | solution.py:49
  (12 shorter events, 0.2 us)
Async XLA Ops:
  7.2 349.3 %all-reduce.3.cloned.1.call-start = ((), (), s32[]{:S(2)}) async-start(), calls=%async_computation.2 | async-start | bytes 18874368 | tf_op jit(solution)/shard_map/psum | solution.py:16
  7.9 3.8 copy-start.1
  12.7 9.7 %copy-start.2 = (f32[8192]{0:T(1024)S(1)}, f32[8192]{0:T(1024)}, u32[]{:S(2)}) copy-start(f32[8192]{0:T(1024)} %param.7) | copy-start | bytes 98308
  12.7 466.4 %all-gather.2.cloned.1.call-start = ((), (), s32[]{:S(2)}) async-start(), calls=%async_computation.1 | async-start | bytes 17301504 | tf_op jit(solution)/shard_map/all_gather | solution.py:66
  22.5 14.9 %copy-start.3 = (s32[256]{0:T(256)S(1)}, s32[256]{0:T(256)}, u32[]{:S(2)}) copy-start(s32[256]{0:T(256)} %param.8) | copy-start | bytes 3076
  25.3 2.1 copy-start
  28.3 124.0 %all-to-all-start = ((bf16[256,32,256]{0,2,1:T(8,128)(2,1)}), bf16[256,32,256]{0,2,1:T(8,128)(2,1)}, u32[]{:S(2)}, u32[]{:S(2)}) async-start(bf16[256,32,256]{0,2,1:T(8,128)(2,1)} %bitcast.31), calls=%async_computation | async-start | bytes 8388608 | tf_op jit(solution)/shard_map/all_to_all | solution.py:65
Sparse Core Ops, SparseCore 0:
  12.8 343.5 all-reduce.2
  358.2 120.8 all-gather.1
where the time goes:
time: 504 us; the launch traced here: 498 us
  waiting for transfers between devices  398 us (79%)
  local copies, waits for them, and re-layouts  41.3 us (8%)
  matrix products  22.7 us (5%)
  between operations  14.9 us (3%)
  other arithmetic  13 us (3%)
  starting transfers between devices  8.73 us (2%)
    psum x1, waiting for transfers between devices, spread(): return lax.psum(jnp.where(mine, array, jnp.zeros_like(array)), axis)  198 us
    all_to_all x1, waiting for transfers between devices, shards(): lax.all_to_all(normed, 'tok', split_axis=1, concat_axis=0, tiled=True)  115 us
    all_gather x1, waiting for transfers between devices, shards(): gathered = lax.all_gather(row_block, 'tok', axis=0, tiled=True)  85.5 us
    dot_general x1, matrix products, transposed_product(): lax.dot_general(left, right, (((0,), (0,)), ((), ())), preferred_element_...  12.4 us
    slice x2, local copies, waits for them, and re-layouts, rotate(): odd = values[:, 1::2]  11.7 us
    slice x2, local copies, waits for them, and re-layouts, rotate(): even = values[:, 0::2]  11.7 us
  transfers between devices with their start and end apart: 3, of which 3 were waited for; matrix products, arithmetic and copies ran while one was open for 12% of the time, Pallas kernels for 0%

commit v1 on v0

v1 whole, which is shorter than its diff:
```python
import functools

import jax
import jax.numpy as jnp
from jax import lax
from jax.experimental import pallas as pl
from jax.experimental.pallas import tpu as pltpu
from jax.sharding import Mesh, PartitionSpec as P

HEAD = 128
SEQ = 128


begin_token = 128000
rope_base = 500000.0

NY, NZ, NC = 4, 4, 8
TOK = ("zl", "y", "k")
COL = ("x", "zh")
ALL = TOK + COL
SIZES = {"y": NY, "zl": NZ, "k": 2}
f32, bf16 = jnp.float32, jnp.bfloat16


def send(array, axis, shift):
    n = SIZES[axis]
    return lax.ppermute(array, axis, [(i, (i + shift) % n) for i in range(n)])


together = lax.optimization_barrier


def pick(array, index):
    return lax.dynamic_index_in_dim(array, index, 0, keepdims=False)


def positions(token_ids):
    samples = token_ids.reshape(-1, SEQ)
    index = jnp.arange(SEQ, dtype=jnp.int32)
    starts = jnp.where(samples == begin_token, index[None, :], 0)
    seen = index[None, :] <= index[:, None]
    latest = jnp.max(jnp.where(seen[None], starts[:, None, :], 0), axis=2)
    return (index[None, :] - latest).reshape(-1)


def turns(place):
    dims = jnp.arange(HEAD, dtype=jnp.int32)
    pair = (dims // 2).astype(f32)
    freq = jnp.power(f32(rope_base), -2.0 * pair / HEAD)
    angle = place.astype(f32)[:, None] * freq[None, :]
    sign = jnp.where(dims % 2 == 0, -1.0, 1.0).astype(f32)
    return jnp.cos(angle), jnp.sin(angle) * sign[None, :]


def normalize(hidden, norm_gain):
    wide = hidden.astype(f32)
    meansq = jnp.mean(wide * wide, axis=-1, keepdims=True)
    return (wide * lax.rsqrt(meansq + 1e-05) * norm_gain[None, :]).astype(bf16)


def across(left, right):
    return lax.dot_general(left, right, (((0,), (0,)), ((), ())), preferred_element_type=f32)


def gram_body(role, table, *refs):
    ca, cb, r0a, r0b, r1a, r1b = (ref[...] for ref in refs[:6])
    rest = refs[6:]
    slot = pl.program_id(0)
    half = NZ // 2
    ta, tb = ca.T, cb.T
    dot = functools.partial(jnp.dot, preferred_element_type=f32)
    tile = jnp.concatenate([dot(ta, r0a) + dot(tb, r0b), dot(ta, r1a) + dot(tb, r1b)], axis=1)
    if role == "far":
        low, high = rest

        @pl.when(slot < half)
        def _():
            low[0] = tile.astype(bf16)

        @pl.when(slot >= half)
        def _():
            high[0] = tile.astype(bf16)

    elif role in ("up", "down"):
        add, out = rest
        use = slot < half if role == "up" else slot >= half
        out[0] = (tile + jnp.where(use, add[0].astype(f32), 0.0)).astype(bf16)
    else:
        first, second, own, others = rest
        tile = tile + first[0].astype(f32) + second[0].astype(f32)

        @pl.when(slot == 0)
        def _():
            own[...] = tile

        @pl.when(slot > 0)
        def _():
            others[0] = tile.astype(bf16)


def gram(role, table, mine, other, *adds):
    tokens, depth = mine.shape
    tile = depth // (NY * NZ * 2)
    half = NZ // 2
    at = lambda row: pl.BlockSpec((tokens, tile), lambda s, tab: (0, tab[row, s]))
    block = (1, tile, 2 * tile)
    low = lambda s, tab: (jnp.minimum(s, half - 1), 0, 0)
    high = lambda s, tab: (jnp.maximum(s - half, 0), 0, 0)
    every = lambda s, tab: (s, 0, 0)
    shape = lambda n, kind: jax.ShapeDtypeStruct((n, tile, 2 * tile), kind)
    ins = [at(0), at(0), at(1), at(1), at(2), at(2)]
    if role == "far":
        outs = [pl.BlockSpec(block, low), pl.BlockSpec(block, high)]
        shapes = [shape(half, bf16), shape(half, bf16)]
    elif role in ("up", "down"):
        ins.append(pl.BlockSpec(block, low if role == "up" else high))
        outs, shapes = pl.BlockSpec(block, every), shape(NZ, bf16)
    else:
        ins += [pl.BlockSpec(block, every)] * 2
        outs = [
            pl.BlockSpec((tile, 2 * tile), lambda s, tab: (0, 0)),
            pl.BlockSpec(block, lambda s, tab: (jnp.maximum(s - 1, 0), 0, 0)),
        ]
        shapes = [jax.ShapeDtypeStruct((tile, 2 * tile), f32), shape(NZ - 1, bf16)]
    return pl.pallas_call(
        functools.partial(gram_body, role),
        grid_spec=pltpu.PrefetchScalarGridSpec(
            num_scalar_prefetch=1, grid=(NZ,), in_specs=ins, out_specs=outs
        ),
        out_shape=shapes,
        cost_estimate=pl.CostEstimate(
            flops=2 * 2 * tokens * 2 * tile * tile * NZ,
            bytes_accessed=8 * NZ * tokens * tile * 2,
            transcendentals=0,
        ),
        name="gram_" + role,
    )(table, mine, other, mine, other, mine, other, *adds)


def project_body(fresh, table, ma, mb, w, *refs):
    out = refs[-1]

    @pl.when(pl.program_id(0) == 0)
    def _():
        out[...] = jnp.zeros_like(out) if fresh else refs[0][...]

    out[0] += jnp.dot(ma[...], w[0], preferred_element_type=f32)
    out[1] += jnp.dot(mb[...], w[0], preferred_element_type=f32)


def project(table, mine, other, weights, sofar=None):
    tokens = mine.shape[0]
    n, piece, width = weights.shape
    at = pl.BlockSpec((tokens, piece), lambda s, tab: (0, tab[s]))
    whole = pl.BlockSpec((2, tokens, width), lambda s, tab: (0, 0, 0))
    fresh = sofar is None
    return pl.pallas_call(
        functools.partial(project_body, fresh),
        grid_spec=pltpu.PrefetchScalarGridSpec(
            num_scalar_prefetch=1,
            grid=(n,),
            in_specs=[at, at, pl.BlockSpec((1, piece, width), lambda s, tab: (s, 0, 0))]
            + ([] if fresh else [whole]),
            out_specs=whole,
        ),
        out_shape=jax.ShapeDtypeStruct((2, tokens, width), f32),
        cost_estimate=pl.CostEstimate(
            flops=4 * tokens * piece * width * n,
            bytes_accessed=n * (2 * tokens * piece + piece * width) * 2 + 16 * tokens * width,
            transcendentals=0,
        ),
        name="project",
    )(table, mine, other, weights, *([] if fresh else [sofar]))


def rope_body(a, b, cosine, sine, out):
    even = lax.broadcasted_iota(jnp.int32, cosine.shape, 1) % 2 == 0
    for start in range(0, a.shape[1], HEAD):
        span = pl.ds(start, HEAD)
        x = a[:, span] + b[:, span]
        swapped = jnp.where(even, pltpu.roll(x, HEAD - 1, 1), pltpu.roll(x, 1, 1))
        out[:, span] = (x * cosine[...] + swapped * sine[...]).astype(out.dtype)


def rope(a, b, cosine, sine):
    return pl.pallas_call(
        rope_body, out_shape=jax.ShapeDtypeStruct(a.shape, bf16), name="rope"
    )(a, b, cosine, sine)


def assemble_body(scale, slots, own, r0, r1, extra, out):
    tile = out.shape[1]

    def put(n, value):
        out[pl.ds(pl.multiple_of(slots[n] * tile, tile), tile), :] = value * scale

    put(0, r1[...].astype(f32))
    put(1, extra[...])
    put(2, r0[...].astype(f32))
    put(3, own[:, :tile].T)
    put(4, own[:, tile:].T)


def assemble(scale, slots, own, r0, r1, extra):
    tile = own.shape[0]
    return pl.pallas_call(
        functools.partial(assemble_body, scale),
        in_specs=[pl.BlockSpec(memory_space=pltpu.SMEM)] + [pl.BlockSpec(memory_space=pltpu.VMEM)] * 4,
        out_shape=jax.ShapeDtypeStruct((4 * tile, tile), f32),
        name="assemble",
    )(slots, own, r0, r1, extra)


def row_pair(t, c):
    u, m = t // 4, t % 4
    p = (t + (c > u)) % 2
    return jnp.where(c == u, m, p), jnp.where(c == u, (m + 1) % 4, p + 2)


def partner_moves(q):
    moves = []
    for t in range(NY * NZ * 2):
        for c in range(NC):
            u, m = t // 4, t % 4
            if c == u:
                r = (m + 1) % 4 if q == 0 else m
            else:
                r = (t + (c > u)) % 2 + 2 * ((q + m // 2) % 2)
            moves.append((t * NC + c, (4 * c + r) * NC + u))
    return moves


def shards(hidden, norm_gain, token_ids, owner, query_store, key_store):
    y, z, k = lax.axis_index("y"), lax.axis_index("zl"), lax.axis_index("k")
    column = lax.axis_index("x") * 2 + lax.axis_index("zh")
    root = owner[0]
    root_z, root_y, root_k = root // 8, (root // 2) % 4, root % 2

    tokens, depth = hidden.shape
    half = depth // 2
    piece = half // (NY * NZ)
    qwidth, kwidth = query_store.shape[2], key_store.shape[2]
    h = NZ // 2
    here = root_k == k

    q = query_store[0].reshape(2 * NY, NZ * piece, qwidth)

    def block(rel, here):
        at = (y + rel) % NY
        there = send(pick(q, (1 - k) * NY + at), "k", 1)
        return jnp.where(here, pick(q, k * NY + at), there)

    step_y = (y - root_y) % NY
    far = block(2, here).reshape(2, h * piece, qwidth)
    far, then = together((far, here))
    a = send(far[0], "y", 1)
    b = send(far[1], "y", -1)
    up = block(1, then).reshape(2, h * piece, qwidth)
    down = block(3, then).reshape(2, h * piece, qwidth)
    c = send(jnp.where(step_y == 1, a[None], up), "y", 1)
    d = send(jnp.where(step_y == 3, b[None], down), "y", -1)
    own = block(0, then).reshape(2, h * piece, qwidth)
    low = lax.broadcasted_iota(jnp.int32, (2, 1, 1), 0) == 0
    from_c = (step_y == 1) | ((step_y == 2) & low)
    quarter = jnp.where(step_y == 0, own, jnp.where(from_c, c, d))
    quarter = quarter.reshape(NZ, piece, qwidth)

    kt = key_store[0].T.reshape(kwidth, 2, half)
    away = jnp.where(k == 0, kt[:, 1], kt[:, 0])
    home = jnp.where(k == 0, kt[:, 0], kt[:, 1])
    wk = jnp.where(here, home, send(away, "k", 1))
    wk = lax.psum(jnp.where((step_y == 0) & (z == root_z), wk, 0), ("zl", "y"))

    mine = normalize(hidden, norm_gain)
    other = send(mine, "k", 1)

    zs = (z + jnp.arange(NZ)) % NZ

    def table(rel):
        t = zs * (2 * NY) + ((y + rel) % NY) * 2 + k
        r0, r1 = row_pair(t, column)
        return jnp.stack([t, 4 * column + r0, 4 * column + r1]).astype(jnp.int32)

    tile = depth // (NY * NZ * 2)
    both = [lax.dynamic_slice_in_dim(x, (4 * column + k) * tile, 3 * tile, 1) for x in (mine, other)]
    extra = sum(across(x[:, :tile], x[:, 2 * tile :]) for x in both)
    p_low, p_high = gram("far", table(2), mine, other)
    p_low, p_high, quarter, extra = together((p_low, p_high, quarter, extra))
    extra = lax.psum(extra, ("zl", "y"))
    ga = send(p_low, "y", 1)
    gb = send(p_high, "y", -1)
    gc = send(gram("up", table(1), mine, other, ga), "y", 1)
    gd = send(gram("down", table(3), mine, other, gb), "y", -1)

    step_z = (z - root_z) % NZ
    seed = pick(quarter, z)
    for s in (1, 2, 3):
        got = send(pick(quarter, (z + s) % NZ), "zl", s)
        seed = jnp.where(step_z == s, got, seed)
    strip = jnp.stack([seed] + [send(seed, "zl", -s) for s in (1, 2, 3)], axis=0)

    hess, rest = gram("own", table(0), mine, other, gc, gd)
    strip, hess, rest = together((strip, hess, rest))

    def depth_tiles(rel):
        return (k * NY * NZ + ((y + rel) % NY) * NZ + zs).astype(jnp.int32)

    left = send(strip, "y", 1)
    right = send(strip, "y", -1)
    raw = project(depth_tiles(0), mine, other, strip)
    parts = [send(rest[s - 1], "zl", s) for s in (1, 2, 3)]
    left, right, parts, extra, wk, raw = together((left, right, parts, extra, wk, raw))
    fl = send(left[:h], "y", 1)
    fr = send(right[h:], "y", -1)

    for part in parts:
        hess = hess + part.astype(f32)
    t = z * (2 * NY) + y * 2 + k
    u, m = t // 4, t % 4
    diagonal = column == u
    r0, r1 = row_pair(t, column)
    tiles = hess.astype(bf16)
    tiles = [tiles[:, :tile], tiles[:, tile:]]
    mirrored = []
    for n in (0, 1):
        second = jnp.where(diagonal, 1, (n + m // 2) % 2) == 1
        mirrored.append(lax.ppermute(jnp.where(second, tiles[1], tiles[0]), ALL, partner_moves(n)))
    missing = 1 - r0 % 2
    slot0 = jnp.where(diagonal, (m + 3) % 4, missing + 2 * ((m // 2) % 2))
    slot1 = jnp.where(diagonal, (m + 2) % 4, missing + 2 * ((m // 2 + 1) % 2))
    slots = jnp.stack([slot1, jnp.where(diagonal, slot1, r0), slot0, r0, r1]).astype(jnp.int32)
    extra = jnp.where(m < 2, extra.T, extra)
    all_tokens = tokens * NY * NZ * 2
    hessian = assemble(2.0 / all_tokens, slots, hess, mirrored[0], mirrored[1], extra)

    raw = project(depth_tiles(3), mine, other, left, raw)
    raw = project(depth_tiles(1), mine, other, right, raw)
    raw = project(depth_tiles(2), mine, other, jnp.concatenate([fl, fr], axis=0), raw)
    cosine, sine = turns(positions(token_ids))
    queries = rope(raw[0], send(raw[1], "k", 1), cosine, sine)

    def keys_of(x):
        x = lax.dynamic_slice_in_dim(x, k * half, half, 1)
        return lax.dot_general(x, wk, (((1,), (1,)), ((), ())), preferred_element_type=f32)

    at = (column * kwidth) % HEAD
    whole = lambda x: jnp.concatenate([x] * (HEAD // kwidth), axis=1)
    keys = rope(whole(keys_of(mine)), whole(send(keys_of(other), "k", 1)), cosine, sine)
    keys = lax.dynamic_slice_in_dim(keys, at, kwidth, 1)
    return (queries, keys, hessian)


def solution(mesh):
    fine = Mesh(mesh.devices.reshape(NZ, NY, 2, 4, 2), ALL)
    placed = (P(TOK, None), P(), P(TOK), P(), P(TOK, None, COL), P(TOK, None, COL))
    return jax.shard_map(
        shards,
        mesh=fine,
        in_specs=placed,
        out_specs=(P(TOK, COL), P(TOK, COL), P(COL, TOK)),
        check_vma=False,
    )
```

time: 504 us -> 515 us (1.022)
  waiting for transfers between devices: 398 us -> 337 us
  Pallas kernels: 0 us -> 49 us
  starting transfers between devices: 8.73 us -> 47.2 us
  local copies, waits for them, and re-layouts: 41.3 us -> 18.3 us
  other arithmetic: 13 us -> 35.2 us
  matrix products: 22.7 us -> 7.77 us
    all_to_all x1 -> x0, waiting for transfers between devices: 115 us -> none  [shards(): lax.all_to_all(normed, 'tok', split_axis=1, concat_axis=0, tiled=True)]
    all_gather x1 -> x0, waiting for transfers between devices: 85.5 us -> none  [shards(): gathered = lax.all_gather(row_block, 'tok', axis=0, tiled=True)]
    psum x1 -> x2, waiting for transfers between devices: 198 us -> 281 us  [the longest x1 161 us: shards(): extra = lax.psum(extra, ('zl', 'y'))]
    ppermute x0 -> x31, waiting for transfers between devices: none -> 56.1 us  [the longest x29 56.1 us: send(): return lax.ppermute(array, axis, [(i, (i + shift) % n) for i in range(n)])]
    pallas_call x0 -> x11, Pallas kernels: none -> 49 us  [the longest x4 21.7 us: gram(): pl.pallas_call(functools.partial(gram_body, role), grid_spec=pltpu.Prefet...]
    ppermute x0 -> x31, starting transfers between devices: none -> 47.1 us  [the longest x29 38.1 us: send(): return lax.ppermute(array, axis, [(i, (i + shift) % n) for i in range(n)])]
    slice x6 -> x2, local copies, waits for them, and re-layouts: 23.7 us -> 0.87 us  [the longest x1 0.83 us: shards(): fr = send(right[h:], 'y', -1)]
    dot_general x3 -> x4, matrix products: 22.7 us -> 7.77 us  [the longest x2 4.65 us: keys_of(): lax.dot_general(x, wk, (((1,), (1,)), ((), ())), preferred_element_type=f32)]
  transfers between devices with their start and end apart: 3 -> 33, of which waited for: 3 -> 8; matrix products, arithmetic and copies ran while one was open for 12% -> 10% of each run, Pallas kernels for 0% -> 9%
where the time goes in v1:
time: 515 us; the launch traced here: 510 us
  waiting for transfers between devices  337 us (65%)
  Pallas kernels  49 us (10%)
  starting transfers between devices  47.2 us (9%)
  other arithmetic  35.2 us (7%)
  local copies, waits for them, and re-layouts  18.3 us (4%)
  between operations  15.2 us (3%)
  matrix products  7.77 us (2%)
    psum x1, waiting for transfers between devices, shards(): extra = lax.psum(extra, ('zl', 'y'))  161 us
    psum x1, waiting for transfers between devices, shards(): wk = lax.psum(jnp.where((step_y == 0) & (z == root_z), wk, 0), ('zl', 'y'))  120 us
    ppermute x29, waiting for transfers between devices, send(): return lax.ppermute(array, axis, [(i, (i + shift) % n) for i in range(n)])  56.1 us
    ppermute x29, starting transfers between devices, send(): return lax.ppermute(array, axis, [(i, (i + shift) % n) for i in range(n)])  38.1 us
    pallas_call x4, Pallas kernels, gram(): pl.pallas_call(functools.partial(gram_body, role), grid_spec=pltpu.Prefet...  21.7 us
    pallas_call x4, Pallas kernels, project(): pl.pallas_call(functools.partial(project_body, fresh), grid_spec=pltpu.Pr...  20.8 us
  transfers between devices with their start and end apart: 33, of which 8 were waited for; matrix products, arithmetic and copies ran while one was open for 10% of the time, Pallas kernels for 9%

profile of v1, /device:TPU:132, one launch (start us, length us, event | category | flops | bytes accessed | tf_op | source)
XLA Modules:
  0.0 509.8 jit_solution(1598311407776053670)
XLA Ops:
  7.3 4.4 dynamic-slice_bitcast_fusion
  13.7 3.2 fusion.2.refs_0_.refs_2_.refs_4_.ma
  18.5 2.5 broadcast_select_fusion.1
  21.0 1.7 bitcast_select_fusion.3
  23.8 1.6 collective-permute-start.3
  27.0 1.7 collective-permute-start.6
  28.7 3.1 bitcast_select_fusion
  31.8 7.5 %collective-permute-done.3 = bf16[512,512]{1,0:T(8,128)(2,1)} collective-permute-done((bf16[512,512]{1,0:T(8,128)(2,1)}, bf16[512,512]{1,0:T(8,128)(2,1)}, u32[]{:S(2)}, u32[]{:S(2)}) %collective-permute-start.3) | collective-permute-done | bytes 524320 | tf_op jit(solution)/shard_map/ppermute | solution.py:27
  39.3 2.1 broadcast_select_fusion.3
  42.8 2.9 collective-permute-start.8
  48.8 18.5 %collective-permute-done.5 = bf16[2,512,512]{2,1,0:T(8,128)(2,1)} collective-permute-done((bf16[2,512,512]{2,1,0:T(8,128)(2,1)}, bf16[2,512,512]{2,1,0:T(8,128)(2,1)}, u32[]{:S(2)}, u32[]{:S(2)}) %collective-permute-start.5) | collective-permute-done | bytes 1048608 | tf_op jit(solution)/shard_map/ppermute | solution.py:27
  69.0 1.7 select_select_fusion
  70.7 1.9 convolution_add_fusion
  72.7 5.3 %gram_far.1 = (bf16[2,256,512]{2,1,0:T(8,128)(2,1)}, bf16[2,256,512]{2,1,0:T(8,128)(2,1)}) custom-call(s32[3,4]{1,0:T(4,128)} %pad_add_fusion.table, bf16[256,8192]{1,0:T(8,128)(2,1)} %fusion.2.refs_0_.refs_2_.refs_4_.ma, bf16[256,8192]{1,0:T(8,128)(2,1)} %collective-permute-done.refs_1_.refs_3_.refs_5_.mb, ...), custom_call_target="tpu_custom_call" | custom-call | flops 536870912 | bytes 4194304 | tf_op jit(solution)/shard_map/gram_far/pallas_call | solution.py:125
  80.9 3.6 collective-permute-start.17
  85.8 2.0 collective-permute-start.9
  89.0 2.1 collective-permute-start.15
  91.7 6.8 %collective-permute-done.10 = bf16[256,512]{1,0:T(8,128)(2,1)} collective-permute-done((bf16[256,512]{1,0:T(8,128)(2,1)}, bf16[256,512]{1,0:T(8,128)(2,1)}, u32[]{:S(2)}, u32[]{:S(2)}) %collective-permute-start.10) | collective-permute-done | bytes 262176 | tf_op jit(solution)/shard_map/ppermute | solution.py:27
  99.5 6.2 %collective-permute-start.14 = (bf16[256,512]{1,0:T(8,128)(2,1)S(1)}, bf16[256,512]{1,0:T(8,128)(2,1)}, u32[]{:S(2)}, u32[]{:S(2)}) collective-permute-start(bf16[256,512]{1,0:T(8,128)(2,1)S(1)} %fusion.9), channel_id=1, source_target_pairs={{0,64},{64,128},{128,192},{192,0},{1,65},{65,129},{129,193},{193,1... | collective-permute-start | bytes 786440 | tf_op jit(solution)/shard_map/ppermute | solution.py:27
  105.9 2.2 collective-permute-start.12
  108.2 5.3 %gram_down.1 = bf16[4,256,512]{2,1,0:T(8,128)(2,1)} custom-call(s32[3,4]{1,0:T(4,128)} %pad_add_fusion.3.table, bf16[256,8192]{1,0:T(8,128)(2,1)} %fusion.2.refs_0_.refs_2_.refs_4_.ma, bf16[256,8192]{1,0:T(8,128)(2,1)} %collective-permute-done.refs_1_.refs_3_.refs_5_.mb, bf16[256,8192]{1,0:T(8,128)(2,1)} %fusion.2.refs_0_.refs_2_.refs_4_.ma, ...), custom_call_target="tpu_custom_call" | custom-call | flops 536870912 | bytes 4194304 | tf_op jit(solution)/shard_map/gram_down/pallas_call | solution.py:125
  113.5 3.7 collective-permute-start.18
  117.2 5.3 %gram_up.1 = bf16[4,256,512]{2,1,0:T(8,128)(2,1)} custom-call(s32[3,4]{1,0:T(4,128)} %pad_add_fusion.2.table, bf16[256,8192]{1,0:T(8,128)(2,1)} %fusion.2.refs_0_.refs_2_.refs_4_.ma, bf16[256,8192]{1,0:T(8,128)(2,1)} %collective-permute-done.refs_1_.refs_3_.refs_5_.mb, bf16[256,8192]{1,0:T(8,128)(2,1)} %fusion.2.refs_0_.refs_2_.refs_4_.ma, ...), custom_call_target="tpu_custom_call" | custom-call | flops 536870912 | bytes 4194304 | tf_op jit(solution)/shard_map/gram_up/pallas_call | solution.py:125
  122.6 2.5 fusion.7
  126.5 13.4 %collective-permute-done.18.refs_7_ = bf16[4,256,512]{2,1,0:T(8,128)(2,1)S(1)} collective-permute-done((bf16[4,256,512]{2,1,0:T(8,128)(2,1)}, bf16[4,256,512]{2,1,0:T(8,128)(2,1)S(1)}, u32[]{:S(2)}, u32[]{:S(2)}) %collective-permute-start.18) | collective-permute-done | bytes 1048608 | tf_op jit(solution)/shard_map/ppermute | solution.py:27
  139.9 9.1 %collective-permute-done.16.refs_6_ = bf16[4,256,512]{2,1,0:T(8,128)(2,1)} collective-permute-done((bf16[4,256,512]{2,1,0:T(8,128)(2,1)}, bf16[4,256,512]{2,1,0:T(8,128)(2,1)}, u32[]{:S(2)}, u32[]{:S(2)}) %collective-permute-start.16) | collective-permute-done | bytes 1048608 | tf_op jit(solution)/shard_map/ppermute | solution.py:27
  149.1 5.6 %gram_own.1 = (f32[256,512]{1,0:T(8,128)}, bf16[3,256,512]{2,1,0:T(8,128)(2,1)}) custom-call(s32[3,4]{1,0:T(4,128)} %pad_add_fusion.1.table, bf16[256,8192]{1,0:T(8,128)(2,1)} %fusion.2.refs_0_.refs_2_.refs_4_.ma, bf16[256,8192]{1,0:T(8,128)(2,1)} %collective-permute-done.refs_1_.refs_3_.refs_5_.mb, bf16[256,8192]{1,0:T(8,128)(2,1)} %fusion.2.refs_0_.refs_2_.refs_4_.ma, ...), custom_call_target="tpu_custom_call" | custom-call | flops 536870912 | bytes 4194304 | tf_op jit(solution)/shard_map/gram_own/pallas_call | solution.py:125
  154.9 1.9 collective-permute-start.19
  156.9 2.0 slice_bitcast_fusion.4
  160.4 1.7 collective-permute-start.21
  163.4 4.9 project.4.refs_0_
  168.2 119.6 %all-reduce.5.cloned.1.call-done = bf16[64,4096]{1,0:T(8,128)(2,1)} async-done(((bf16[64,4096]{1,0:T(8,128)(2,1)}), bf16[64,4096]{1,0:T(8,128)(2,1)}) %all-reduce.5.cloned.1.call-update) | async-done | bytes 524304 | tf_op jit(solution)/shard_map/psum | solution.py:272
  287.8 161.4 %all-reduce.3.cloned.1.call-done = f32[256,256]{1,0:T(8,128)} async-done(((f32[256,256]{1,0:T(8,128)}), f32[256,256]{1,0:T(8,128)}) %all-reduce.3.cloned.1.call-update) | async-done | bytes 262160 | tf_op jit(solution)/shard_map/psum | solution.py:289
  450.1 2.4 fusion.3
  452.8 2.0 collective-permute-start.25
  454.8 2.3 fusion.46
  457.8 1.9 collective-permute-start.30
  459.7 7.1 %collective-permute-start.29 = (bf16[256,256]{1,0:T(8,128)(2,1)}, bf16[256,256]{1,0:T(8,128)(2,1)S(1)}, u32[]{:S(2)}, u32[]{:S(2)}) collective-permute-start(bf16[256,256]{1,0:T(8,128)(2,1)} %get-tuple-element.98), channel_id=1, source_target_pairs={{0,8},{1,40},{2,72},{3,104},{4,136},{5,168},{6,200},{7,232},{8,16}... | collective-permute-start | bytes 393224 | tf_op jit(solution)/shard_map/ppermute | solution.py:327
  466.8 5.3 %project.5.refs_0_ = f32[2,256,512]{2,1,0:T(8,128)} custom-call(s32[4]{0:T(128)} %broadcast_add_fusion.table, bf16[256,8192]{1,0:T(8,128)(2,1)} %fusion.2.refs_0_.refs_2_.refs_4_.ma, bf16[256,8192]{1,0:T(8,128)(2,1)} %collective-permute-done.refs_1_.refs_3_.refs_5_.mb, bf16[4,256,512]{2,1,0:T(8,128)(2,1)} %copy-done.3, f32[2,256,512]{2,1,0:T(8,128)} %project.4.refs_0_), custom_call_target="tpu_custom_call" | custom-call | flops 536870912 | bytes 4194304 | tf_op jit(solution)/shard_map/project/pallas_call | solution.py:157
  472.1 5.3 %project.6.refs_0_ = f32[2,256,512]{2,1,0:T(8,128)} custom-call(s32[4]{0:T(128)} %get-tuple-element.107.table, bf16[256,8192]{1,0:T(8,128)(2,1)} %fusion.2.refs_0_.refs_2_.refs_4_.ma, bf16[256,8192]{1,0:T(8,128)(2,1)} %collective-permute-done.refs_1_.refs_3_.refs_5_.mb, bf16[4,256,512]{2,1,0:T(8,128)(2,1)} %copy-done.2, f32[2,256,512]{2,1,0:T(8,128)} %project.5.refs_0_), custom_call_target="tpu_custom_call" | custom-call | flops 536870912 | bytes 4194304 | tf_op jit(solution)/shard_map/project/pallas_call | solution.py:157
  478.1 2.3 pad_maximum_fusion.1.w
  480.4 5.4 %project.7 = f32[2,256,512]{2,1,0:T(8,128)} custom-call(s32[4]{0:T(128)} %get-tuple-element.108.table, bf16[256,8192]{1,0:T(8,128)(2,1)} %fusion.2.refs_0_.refs_2_.refs_4_.ma, bf16[256,8192]{1,0:T(8,128)(2,1)} %collective-permute-done.refs_1_.refs_3_.refs_5_.mb, bf16[4,256,512]{2,1,0:T(8,128)(2,1)} %pad_maximum_fusion.1.w, f32[2,256,512]{2,1,0:T(8,128)} %project.6.refs_0_), custom_call_target="tpu_custom_call" | custom-call | flops 536870912 | bytes 4194304 | tf_op jit(solution)/shard_map/project/pallas_call | solution.py:157
  485.8 2.1 slice_bitcast_fusion
  488.4 2.3 fusion.5
  491.5 1.7 pad_maximum_fusion.3.b
  493.2 1.9 rope.3
  497.4 2.4 assemble.1
  500.6 2.3 rope.2
  (119 shorter events, 30.5 us)
Async XLA Ops:
  7.2 280.7 %all-reduce.5.cloned.1.call-start = ((), (), s32[]{:S(2)}) async-start(), calls=%async_computation.1 | async-start | bytes 1048576 | tf_op jit(solution)/shard_map/psum | solution.py:272
  7.3 5.4 %copy-start = (bf16[256,8192]{1,0:T(8,128)(2,1)S(1)}, bf16[256,8192]{1,0:T(8,128)(2,1)}, u32[]{:S(2)}) copy-start(bf16[256,8192]{1,0:T(8,128)(2,1)} %param.6) | copy-start | bytes 12582916
  11.7 2.0 copy-start.14
  11.7 15.1 %collective-permute-start.7 = (bf16[1024,512]{1,0:T(8,128)(2,1)}, bf16[1024,512]{1,0:T(8,128)(2,1)}, u32[]{:S(2)}, u32[]{:S(2)}) collective-permute-start(bf16[1024,512]{1,0:T(8,128)(2,1)} %get-tuple-element.81), channel_id=1, source_target_pairs={{0,8},{8,0},{1,9},{9,1},{2,10},{10,2},{3,11},{11,3},{4,12},{12,4},... | collective-permute-start | bytes 3145736 | tf_op jit(solution)/shard_map/ppermute | solution.py:27
  11.7 15.2 %collective-permute-start.4 = (bf16[1024,512]{1,0:T(8,128)(2,1)}, bf16[1024,512]{1,0:T(8,128)(2,1)}, u32[]{:S(2)}, u32[]{:S(2)}) collective-permute-start(bf16[1024,512]{1,0:T(8,128)(2,1)} %get-tuple-element.82), channel_id=1, source_target_pairs={{0,8},{8,0},{1,9},{9,1},{2,10},{10,2},{3,11},{11,3},{4,12},{12,4},... | collective-permute-start | bytes 3145736 | tf_op jit(solution)/shard_map/ppermute | solution.py:27
  12.2 16.5 %collective-permute-start.2 = (bf16[1024,512]{1,0:T(8,128)(2,1)}, bf16[1024,512]{1,0:T(8,128)(2,1)}, u32[]{:S(2)}, u32[]{:S(2)}) collective-permute-start(bf16[1024,512]{1,0:T(8,128)(2,1)} %get-tuple-element.83), channel_id=1, source_target_pairs={{0,8},{8,0},{1,9},{9,1},{2,10},{10,2},{3,11},{11,3},{4,12},{12,4},... | collective-permute-start | bytes 3145736 | tf_op jit(solution)/shard_map/ppermute | solution.py:27
  12.3 8.7 %collective-permute-start.1 = (bf16[1024,512]{1,0:T(8,128)(2,1)}, bf16[1024,512]{1,0:T(8,128)(2,1)}, u32[]{:S(2)}, u32[]{:S(2)}) collective-permute-start(bf16[1024,512]{1,0:T(8,128)(2,1)} %get-tuple-element.84), channel_id=1, source_target_pairs={{0,8},{8,0},{1,9},{9,1},{2,10},{10,2},{3,11},{11,3},{4,12},{12,4},... | collective-permute-start | bytes 3145736 | tf_op jit(solution)/shard_map/ppermute | solution.py:27
  13.7 4.0 copy-start.7
  16.8 53.9 %collective-permute-start = (bf16[256,8192]{1,0:T(8,128)(2,1)}, bf16[256,8192]{1,0:T(8,128)(2,1)}, u32[]{:S(2)}, u32[]{:S(2)}) collective-permute-start(bf16[256,8192]{1,0:T(8,128)(2,1)} %fusion.2.refs_0_.refs_2_.refs_4_.ma), channel_id=1, source_target_pairs={{0,8},{8,0},{1,9},{9,1},{2,10},{10,2},{3,11},{11,3},{4,12},{12,4},... | collective-permute-start | bytes 12582920 | tf_op jit(solution)/shard_map/ppermute | solution.py:27
  23.8 15.5 %collective-permute-start.3 = (bf16[512,512]{1,0:T(8,128)(2,1)}, bf16[512,512]{1,0:T(8,128)(2,1)}, u32[]{:S(2)}, u32[]{:S(2)}) collective-permute-start(bf16[512,512]{1,0:T(8,128)(2,1)} %get-tuple-element.93), channel_id=1, source_target_pairs={{0,16},{16,32},{32,48},{48,0},{1,17},{17,33},{33,49},{49,1},{2,18}... | collective-permute-start | bytes 1572872 | tf_op jit(solution)/shard_map/ppermute | solution.py:27
  26.8 95.7 %collective-permute-start.24 = (bf16[64,4096]{1,0:T(8,128)(2,1)}, bf16[64,4096]{1,0:T(8,128)(2,1)}, u32[]{:S(2)}, u32[]{:S(2)}) collective-permute-start(bf16[64,4096]{1,0:T(8,128)(2,1)} %bitcast.74), channel_id=1, source_target_pairs={{0,8},{8,0},{1,9},{9,1},{2,10},{10,2},{3,11},{11,3},{4,12},{12,4},... | collective-permute-start | bytes 1572872 | tf_op jit(solution)/shard_map/ppermute | solution.py:27
  27.0 14.8 %collective-permute-start.6 = (bf16[512,512]{1,0:T(8,128)(2,1)}, bf16[512,512]{1,0:T(8,128)(2,1)S(1)}, u32[]{:S(2)}, u32[]{:S(2)}) collective-permute-start(bf16[512,512]{1,0:T(8,128)(2,1)} %get-tuple-element.92), channel_id=1, source_target_pairs={{0,48},{16,0},{32,16},{48,32},{1,49},{17,1},{33,17},{49,33},{2,50}... | collective-permute-start | bytes 1572872 | tf_op jit(solution)/shard_map/ppermute | solution.py:27
  41.4 25.9 %collective-permute-start.5 = (bf16[2,512,512]{2,1,0:T(8,128)(2,1)}, bf16[2,512,512]{2,1,0:T(8,128)(2,1)}, u32[]{:S(2)}, u32[]{:S(2)}) collective-permute-start(bf16[2,512,512]{2,1,0:T(8,128)(2,1)} %broadcast_select_fusion.3), channel_id=1, source_target_pairs={{0,16},{16,32},{32,48},{48,0},{1,17},{17,33},{33,49},{49,1},{2,18}... | collective-permute-start | bytes 3145736 | tf_op jit(solution)/shard_map/ppermute | solution.py:27
  42.8 25.2 %collective-permute-start.8 = (bf16[2,512,512]{2,1,0:T(8,128)(2,1)}, bf16[2,512,512]{2,1,0:T(8,128)(2,1)S(1)}, u32[]{:S(2)}, u32[]{:S(2)}) collective-permute-start(bf16[2,512,512]{2,1,0:T(8,128)(2,1)} %broadcast_select_fusion.2), channel_id=1, source_target_pairs={{0,48},{16,0},{32,16},{48,32},{1,49},{17,1},{33,17},{49,33},{2,50}... | collective-permute-start | bytes 3145736 | tf_op jit(solution)/shard_map/ppermute | solution.py:27
  68.0 1.0 copy-start.5
  78.8 10.2 %collective-permute-start.11 = (bf16[256,512]{1,0:T(8,128)(2,1)S(1)}, bf16[256,512]{1,0:T(8,128)(2,1)}, u32[]{:S(2)}, u32[]{:S(2)}) collective-permute-start(bf16[256,512]{1,0:T(8,128)(2,1)S(1)} %get-tuple-element.89), channel_id=1, source_target_pairs={{0,64},{64,128},{128,192},{192,0},{1,65},{65,129},{129,193},{193,1... | collective-permute-start | bytes 786440 | tf_op jit(solution)/shard_map/ppermute | solution.py:27
  80.9 25.0 %collective-permute-start.17 = (bf16[2,256,512]{2,1,0:T(8,128)(2,1)}, bf16[2,256,512]{2,1,0:T(8,128)(2,1)S(1)}, u32[]{:S(2)}, u32[]{:S(2)}) collective-permute-start(bf16[2,256,512]{2,1,0:T(8,128)(2,1)} %get-tuple-element.30), channel_id=1, source_target_pairs={{0,48},{16,0},{32,16},{48,32},{1,49},{17,1},{33,17},{49,33},{2,50}... | collective-permute-start | bytes 1572872 | tf_op jit(solution)/shard_map/ppermute | solution.py:27
  84.5 14.0 %collective-permute-start.10 = (bf16[256,512]{1,0:T(8,128)(2,1)}, bf16[256,512]{1,0:T(8,128)(2,1)}, u32[]{:S(2)}, u32[]{:S(2)}) collective-permute-start(bf16[256,512]{1,0:T(8,128)(2,1)} %get-tuple-element.90), channel_id=1, source_target_pairs={{0,128},{64,192},{128,0},{192,64},{1,129},{65,193},{129,1},{193,65... | collective-permute-start | bytes 786440 | tf_op jit(solution)/shard_map/ppermute | solution.py:27
  85.8 12.7 %collective-permute-start.9 = (bf16[256,512]{1,0:T(8,128)(2,1)S(1)}, bf16[256,512]{1,0:T(8,128)(2,1)}, u32[]{:S(2)}, u32[]{:S(2)}) collective-permute-start(bf16[256,512]{1,0:T(8,128)(2,1)S(1)} %get-tuple-element.91), channel_id=1, source_target_pairs={{0,192},{64,0},{128,64},{192,128},{1,193},{65,1},{129,65},{193,129... | collective-permute-start | bytes 786440 | tf_op jit(solution)/shard_map/ppermute | solution.py:27
  89.0 24.5 %collective-permute-start.15 = (bf16[2,256,512]{2,1,0:T(8,128)(2,1)}, bf16[2,256,512]{2,1,0:T(8,128)(2,1)S(1)}, u32[]{:S(2)}, u32[]{:S(2)}) collective-permute-start(bf16[2,256,512]{2,1,0:T(8,128)(2,1)} %get-tuple-element.29), channel_id=1, source_target_pairs={{0,16},{16,32},{32,48},{48,0},{1,17},{17,33},{33,49},{49,1},{2,18}... | collective-permute-start | bytes 1572872 | tf_op jit(solution)/shard_map/ppermute | solution.py:27
  99.5 25.7 %collective-permute-start.14 = (bf16[256,512]{1,0:T(8,128)(2,1)S(1)}, bf16[256,512]{1,0:T(8,128)(2,1)}, u32[]{:S(2)}, u32[]{:S(2)}) collective-permute-start(bf16[256,512]{1,0:T(8,128)(2,1)S(1)} %fusion.9), channel_id=1, source_target_pairs={{0,64},{64,128},{128,192},{192,0},{1,65},{65,129},{129,193},{193,1... | collective-permute-start | bytes 786440 | tf_op jit(solution)/shard_map/ppermute | solution.py:27
  105.7 19.6 %collective-permute-start.13 = (bf16[256,512]{1,0:T(8,128)(2,1)S(1)}, bf16[256,512]{1,0:T(8,128)(2,1)}, u32[]{:S(2)}, u32[]{:S(2)}) collective-permute-start(bf16[256,512]{1,0:T(8,128)(2,1)S(1)} %fusion.9), channel_id=1, source_target_pairs={{0,128},{64,192},{128,0},{192,64},{1,129},{65,193},{129,1},{193,65... | collective-permute-start | bytes 786440 | tf_op jit(solution)/shard_map/ppermute | solution.py:27
  105.9 2.2 copy-start.9
  105.9 19.3 %collective-permute-start.12 = (bf16[256,512]{1,0:T(8,128)(2,1)S(1)}, bf16[256,512]{1,0:T(8,128)(2,1)}, u32[]{:S(2)}, u32[]{:S(2)}) collective-permute-start(bf16[256,512]{1,0:T(8,128)(2,1)S(1)} %fusion.9), channel_id=1, source_target_pairs={{0,192},{64,0},{128,64},{192,128},{1,193},{65,1},{129,65},{193,129... | collective-permute-start | bytes 786440 | tf_op jit(solution)/shard_map/ppermute | solution.py:27
  113.5 3.7 copy-start.10
  113.5 26.4 %collective-permute-start.18 = (bf16[4,256,512]{2,1,0:T(8,128)(2,1)}, bf16[4,256,512]{2,1,0:T(8,128)(2,1)S(1)}, u32[]{:S(2)}, u32[]{:S(2)}) collective-permute-start(bf16[4,256,512]{2,1,0:T(8,128)(2,1)} %gram_down.1), channel_id=1, source_target_pairs={{0,48},{16,0},{32,16},{48,32},{1,49},{17,1},{33,17},{49,33},{2,50}... | collective-permute-start | bytes 3145736 | tf_op jit(solution)/shard_map/ppermute | solution.py:27
  122.6 26.5 %collective-permute-start.16 = (bf16[4,256,512]{2,1,0:T(8,128)(2,1)}, bf16[4,256,512]{2,1,0:T(8,128)(2,1)}, u32[]{:S(2)}, u32[]{:S(2)}) collective-permute-start(bf16[4,256,512]{2,1,0:T(8,128)(2,1)} %gram_up.1), channel_id=1, source_target_pairs={{0,16},{16,32},{32,48},{48,0},{1,17},{17,33},{33,49},{49,1},{2,18}... | collective-permute-start | bytes 3145736 | tf_op jit(solution)/shard_map/ppermute | solution.py:27
  125.2 324.0 %all-reduce.3.cloned.1.call-start = ((), (), s32[]{:S(2)}) async-start(), calls=%async_computation | async-start | bytes 524288 | tf_op jit(solution)/shard_map/psum | solution.py:289
  126.5 28.4 %copy-start.1 = (bf16[4,256,512]{2,1,0:T(8,128)(2,1)}, bf16[4,256,512]{2,1,0:T(8,128)(2,1)S(1)}, u32[]{:S(2)}) copy-start(bf16[4,256,512]{2,1,0:T(8,128)(2,1)S(1)} %pad_maximum_fusion.w) | copy-start | bytes 3145732
  126.5 30.2 %copy-start.15 = (s32[256]{0:T(256)S(1)}, s32[256]{0:T(256)}, u32[]{:S(2)}) copy-start(s32[256]{0:T(256)} %param.8) | copy-start | bytes 3076
  139.9 9.1 %copy-start.6 = (bf16[4,256,512]{2,1,0:T(8,128)(2,1)}, bf16[4,256,512]{2,1,0:T(8,128)(2,1)S(1)}, u32[]{:S(2)}) copy-start(bf16[4,256,512]{2,1,0:T(8,128)(2,1)S(1)} %collective-permute-done.18.refs_7_) | copy-start | bytes 3145732
  154.7 294.5 %collective-permute-start.20 = (bf16[4,256,512]{2,1,0:T(8,128)(2,1)S(1)}, bf16[4,256,512]{2,1,0:T(8,128)(2,1)S(1)}, u32[]{:S(2)}, u32[]{:S(2)}) collective-permute-start(bf16[4,256,512]{2,1,0:T(8,128)(2,1)S(1)} %pad_maximum_fusion.w), channel_id=1, source_target_pairs={{0,48},{16,0},{32,16},{48,32},{1,49},{17,1},{33,17},{49,33},{2,50}... | collective-permute-start | bytes 3145736 | tf_op jit(solution)/shard_map/ppermute | solution.py:27
  154.9 294.3 %collective-permute-start.19 = (bf16[4,256,512]{2,1,0:T(8,128)(2,1)S(1)}, bf16[4,256,512]{2,1,0:T(8,128)(2,1)S(1)}, u32[]{:S(2)}, u32[]{:S(2)}) collective-permute-start(bf16[4,256,512]{2,1,0:T(8,128)(2,1)S(1)} %pad_maximum_fusion.w), channel_id=1, source_target_pairs={{0,16},{16,32},{32,48},{48,0},{1,17},{17,33},{33,49},{49,1},{2,18}... | collective-permute-start | bytes 3145736 | tf_op jit(solution)/shard_map/ppermute | solution.py:27
  158.9 290.2 %collective-permute-start.23 = (bf16[256,512]{1,0:T(8,128)(2,1)}, bf16[256,512]{1,0:T(8,128)(2,1)}, u32[]{:S(2)}, u32[]{:S(2)}) collective-permute-start(bf16[256,512]{1,0:T(8,128)(2,1)} %get-tuple-element.94), channel_id=1, source_target_pairs={{0,192},{64,0},{128,64},{192,128},{1,193},{65,1},{129,65},{193,129... | collective-permute-start | bytes 786440 | tf_op jit(solution)/shard_map/ppermute | solution.py:27
  160.4 288.8 %collective-permute-start.22 = (bf16[256,512]{1,0:T(8,128)(2,1)}, bf16[256,512]{1,0:T(8,128)(2,1)}, u32[]{:S(2)}, u32[]{:S(2)}) collective-permute-start(bf16[256,512]{1,0:T(8,128)(2,1)} %get-tuple-element.95), channel_id=1, source_target_pairs={{0,128},{64,192},{128,0},{192,64},{1,129},{65,193},{129,1},{193,65... | collective-permute-start | bytes 786440 | tf_op jit(solution)/shard_map/ppermute | solution.py:27
  160.4 288.8 %collective-permute-start.21 = (bf16[256,512]{1,0:T(8,128)(2,1)}, bf16[256,512]{1,0:T(8,128)(2,1)}, u32[]{:S(2)}, u32[]{:S(2)}) collective-permute-start(bf16[256,512]{1,0:T(8,128)(2,1)} %get-tuple-element.96), channel_id=1, source_target_pairs={{0,64},{64,128},{128,192},{192,0},{1,65},{65,129},{129,193},{193,1... | collective-permute-start | bytes 786440 | tf_op jit(solution)/shard_map/ppermute | solution.py:27
  449.2 3.4 copy-start.8
  449.2 22.9 %copy-start.2 = (bf16[4,256,512]{2,1,0:T(8,128)(2,1)}, bf16[4,256,512]{2,1,0:T(8,128)(2,1)S(1)}, u32[]{:S(2)}) copy-start(bf16[4,256,512]{2,1,0:T(8,128)(2,1)S(1)} %collective-permute-done.20.w) | copy-start | bytes 3145732
  449.2 17.6 %copy-start.3 = (bf16[4,256,512]{2,1,0:T(8,128)(2,1)}, bf16[4,256,512]{2,1,0:T(8,128)(2,1)S(1)}, u32[]{:S(2)}) copy-start(bf16[4,256,512]{2,1,0:T(8,128)(2,1)S(1)} %collective-permute-done.19.w) | copy-start | bytes 3145732
  452.5 39.0 %collective-permute-start.28 = (f32[256,64]{1,0:T(8,128)S(1)}, f32[256,64]{1,0:T(8,128)}, u32[]{:S(2)}, u32[]{:S(2)}) collective-permute-start(f32[256,64]{1,0:T(8,128)S(1)} %fusion.3), channel_id=1, source_target_pairs={{0,8},{8,0},{1,9},{9,1},{2,10},{10,2},{3,11},{11,3},{4,12},{12,4},... | collective-permute-start | bytes 196616 | tf_op jit(solution)/shard_map/ppermute | solution.py:27
  452.7 25.4 %collective-permute-start.26 = (bf16[2,256,512]{2,1,0:T(8,128)(2,1)}, bf16[2,256,512]{2,1,0:T(8,128)(2,1)}, u32[]{:S(2)}, u32[]{:S(2)}) collective-permute-start(bf16[2,256,512]{2,1,0:T(8,128)(2,1)} %slice.65), channel_id=1, source_target_pairs={{0,48},{16,0},{32,16},{48,32},{1,49},{17,1},{33,17},{49,33},{2,50}... | collective-permute-start | bytes 1572872 | tf_op jit(solution)/shard_map/ppermute | solution.py:27
  452.8 25.3 %collective-permute-start.25 = (bf16[2,256,512]{2,1,0:T(8,128)(2,1)S(1)}, bf16[2,256,512]{2,1,0:T(8,128)(2,1)}, u32[]{:S(2)}, u32[]{:S(2)}) collective-permute-start(bf16[2,256,512]{2,1,0:T(8,128)(2,1)S(1)} %slice.64), channel_id=1, source_target_pairs={{0,16},{16,32},{32,48},{48,0},{1,17},{17,33},{33,49},{49,1},{2,18}... | collective-permute-start | bytes 1572872 | tf_op jit(solution)/shard_map/ppermute | solution.py:27
  457.8 38.9 %collective-permute-start.30 = (bf16[256,256]{1,0:T(8,128)(2,1)}, bf16[256,256]{1,0:T(8,128)(2,1)S(1)}, u32[]{:S(2)}, u32[]{:S(2)}) collective-permute-start(bf16[256,256]{1,0:T(8,128)(2,1)} %get-tuple-element.97), channel_id=1, source_target_pairs={{0,0},{1,56},{2,88},{3,120},{4,152},{5,184},{6,216},{7,248},{8,8},... | collective-permute-start | bytes 393224 | tf_op jit(solution)/shard_map/ppermute | solution.py:327
  459.7 37.0 %collective-permute-start.29 = (bf16[256,256]{1,0:T(8,128)(2,1)}, bf16[256,256]{1,0:T(8,128)(2,1)S(1)}, u32[]{:S(2)}, u32[]{:S(2)}) collective-permute-start(bf16[256,256]{1,0:T(8,128)(2,1)} %get-tuple-element.98), channel_id=1, source_target_pairs={{0,8},{1,40},{2,72},{3,104},{4,136},{5,168},{6,200},{7,232},{8,16}... | collective-permute-start | bytes 393224 | tf_op jit(solution)/shard_map/ppermute | solution.py:327
  480.4 8.1 %copy-start.4 = (bf16[64,4096]{1,0:T(8,128)(2,1)S(1)}, bf16[64,4096]{1,0:T(8,128)(2,1)}, u32[]{:S(2)}) copy-start(bf16[64,4096]{1,0:T(8,128)(2,1)} %all-reduce.5.cloned.1.call-done) | copy-start | bytes 1572868
  487.9 12.0 %collective-permute-start.27 = (f32[256,512]{1,0:T(8,128)S(1)}, f32[256,512]{1,0:T(8,128)S(1)}, u32[]{:S(2)}, u32[]{:S(2)}) collective-permute-start(f32[256,512]{1,0:T(8,128)S(1)} %get-tuple-element.85), channel_id=1, source_target_pairs={{0,8},{8,0},{1,9},{9,1},{2,10},{10,2},{3,11},{11,3},{4,12},{12,4},... | collective-permute-start | bytes 1572872 | tf_op jit(solution)/shard_map/ppermute | solution.py:27
  496.7 0.7 copy-start.13
  499.8 0.8 copy-start.11
  (1 other events, 0.7 us)
Sparse Core Ops, SparseCore 0:
  125.3 162.4 all-reduce.4
  290.6 158.5 all-reduce.2

commit v2 on v1

v2 whole, which is shorter than its diff:
```python
import functools

import jax
import jax.numpy as jnp
from jax import lax
from jax.experimental import pallas as pl
from jax.experimental.pallas import tpu as pltpu
from jax.sharding import Mesh, PartitionSpec as P

HEAD = 128
SEQ = 128


begin_token = 128000
rope_base = 500000.0

NY, NZ, NC = 4, 4, 8
TOK = ("zl", "y", "k")
COL = ("x", "zh")
ALL = TOK + COL
SIZES = {"y": NY, "zl": NZ, "k": 2}
f32, bf16 = jnp.float32, jnp.bfloat16


def send(array, axis, shift):
    n = SIZES[axis]
    return lax.ppermute(array, axis, [(i, (i + shift) % n) for i in range(n)])


together = lax.optimization_barrier


def pick(array, index):
    return lax.dynamic_index_in_dim(array, index, 0, keepdims=False)


def positions(token_ids):
    samples = token_ids.reshape(-1, SEQ)
    index = jnp.arange(SEQ, dtype=jnp.int32)
    starts = jnp.where(samples == begin_token, index[None, :], 0)
    seen = index[None, :] <= index[:, None]
    latest = jnp.max(jnp.where(seen[None], starts[:, None, :], 0), axis=2)
    return (index[None, :] - latest).reshape(-1)


def turns(place):
    dims = jnp.arange(HEAD, dtype=jnp.int32)
    pair = (dims // 2).astype(f32)
    freq = jnp.power(f32(rope_base), -2.0 * pair / HEAD)
    angle = place.astype(f32)[:, None] * freq[None, :]
    sign = jnp.where(dims % 2 == 0, -1.0, 1.0).astype(f32)
    return jnp.cos(angle), jnp.sin(angle) * sign[None, :]


def normalize(hidden, norm_gain):
    wide = hidden.astype(f32)
    meansq = jnp.mean(wide * wide, axis=-1, keepdims=True)
    return (wide * lax.rsqrt(meansq + 1e-05) * norm_gain[None, :]).astype(bf16)


def across(left, right):
    return lax.dot_general(left, right, (((0,), (0,)), ((), ())), preferred_element_type=f32)


def gram_body(table, *refs):
    ca, cb, r0a, r0b, r1a, r1b = (ref[...] for ref in refs[:6])
    low, high, base = refs[6:]
    slot = pl.program_id(0)
    half = NZ // 2
    ta, tb = ca.T, cb.T
    dot = functools.partial(jnp.dot, preferred_element_type=f32)
    tile = jnp.concatenate([dot(ta, r0a) + dot(tb, r0b), dot(ta, r1a) + dot(tb, r1b)], axis=1)

    @pl.when(slot < half)
    def _():
        low[0] = tile.astype(bf16)

    @pl.when((slot >= half) & (slot < NZ))
    def _():
        high[0] = tile.astype(bf16)

    @pl.when(slot >= NZ)
    def _():
        base[0] = tile


def gram(table, mine, other):
    tokens, depth = mine.shape
    n = table.shape[1]
    tile = depth // (NY * NZ * 2)
    half = NZ // 2
    at = lambda row: pl.BlockSpec((tokens, tile), lambda s, tab: (0, tab[row, s]))
    block = (1, tile, 2 * tile)
    shape = lambda n, kind: jax.ShapeDtypeStruct((n, tile, 2 * tile), kind)
    return pl.pallas_call(
        gram_body,
        grid_spec=pltpu.PrefetchScalarGridSpec(
            num_scalar_prefetch=1,
            grid=(n,),
            in_specs=[at(0), at(0), at(1), at(1), at(2), at(2)],
            out_specs=[
                pl.BlockSpec(block, lambda s, tab: (jnp.minimum(s, half - 1), 0, 0)),
                pl.BlockSpec(block, lambda s, tab: (jnp.clip(s - half, 0, half - 1), 0, 0)),
                pl.BlockSpec(block, lambda s, tab: (jnp.maximum(s - NZ, 0), 0, 0)),
            ],
        ),
        out_shape=[shape(half, bf16), shape(half, bf16), shape(n - NZ, f32)],
        cost_estimate=pl.CostEstimate(
            flops=8 * tokens * 2 * tile * tile * n,
            bytes_accessed=8 * n * tokens * tile * 2,
            transcendentals=0,
        ),
        name="gram",
    )(table, mine, other, mine, other, mine, other)


def project_body(slots, piece, fresh, table, *refs):
    out = refs[-1]
    ma, mb = refs[:slots], refs[slots : 2 * slots]
    ws = refs[2 * slots : -1 if fresh else -2]
    width = ws[0].shape[2]
    depth_of = [(w, i) for w in ws for i in range(w.shape[0])]
    keys = []
    for w, i in depth_of:
        kt = w[i, piece:, :]
        kt = [kt[:, :piece], kt[:, piece:]]
        keys.append(jnp.concatenate(kt + kt, axis=0))
    for core, tokens in ((0, ma), (1, mb)):
        main = jnp.zeros(out.shape[1:2] + (width,), f32) if fresh else refs[-2][core, :, :width]
        side = jnp.zeros(out.shape[1:2] + (HEAD,), f32) if fresh else refs[-2][core, :, width:]
        for (w, i), x, kt in zip(depth_of, tokens, keys):
            main += jnp.dot(x[...], w[i, :piece, :], preferred_element_type=f32)
            side += lax.dot_general(
                x[...], kt, (((1,), (1,)), ((), ())), preferred_element_type=f32
            )
        out[core, :, :width] = main
        out[core, :, width:] = side


def project(table, mine, other, weights, sofar=None):
    tokens = mine.shape[0]
    slots = table.shape[0]
    rows, width = weights[0].shape[1:]
    piece = width // 2
    at = [pl.BlockSpec((tokens, piece), lambda s, tab, n=n: (0, tab[n])) for n in range(slots)]
    full = lambda shape: pl.BlockSpec(shape, lambda s, tab: (0, 0, 0))
    whole = (2, tokens, width + HEAD)
    fresh = sofar is None
    return pl.pallas_call(
        functools.partial(project_body, slots, piece, fresh),
        grid_spec=pltpu.PrefetchScalarGridSpec(
            num_scalar_prefetch=1,
            grid=(1,),
            in_specs=at + at + [full(w.shape) for w in weights] + ([] if fresh else [full(whole)]),
            out_specs=full(whole),
        ),
        out_shape=jax.ShapeDtypeStruct(whole, f32),
        cost_estimate=pl.CostEstimate(
            flops=4 * tokens * piece * width * slots,
            bytes_accessed=slots * (2 * tokens * piece + rows * width) * 2 + 16 * tokens * width,
            transcendentals=0,
        ),
        name="project",
    )(table, *[mine] * slots, *[other] * slots, *weights, *([] if fresh else [sofar]))


def rope_body(a, b, cosine, sine, queries, keys):
    even = lax.broadcasted_iota(jnp.int32, cosine.shape, 1) % 2 == 0
    width = queries.shape[1]
    for start in range(0, width + HEAD, HEAD):
        x = a[0, :, start : start + HEAD] + b[:, start : start + HEAD]
        swapped = jnp.where(even, pltpu.roll(x, HEAD - 1, 1), pltpu.roll(x, 1, 1))
        x = (x * cosine[...] + swapped * sine[...]).astype(bf16)
        if start < width:
            queries[:, start : start + HEAD] = x
        else:
            keys[...] = x


def rope(a, b, cosine, sine):
    tokens, width = b.shape
    full = lambda shape: pl.BlockSpec(shape, lambda i: (0,) * len(shape))
    shapes = [(tokens, width - HEAD), (tokens, HEAD)]
    return pl.pallas_call(
        rope_body,
        grid=(1,),
        in_specs=[full((1, tokens, width)), full(b.shape), full(cosine.shape), full(sine.shape)],
        out_specs=[full(shape) for shape in shapes],
        out_shape=[jax.ShapeDtypeStruct(shape, bf16) for shape in shapes],
        name="rope",
    )(a, b, cosine, sine)


def assemble_body(scale, slots, own, r0, r1, extra, out):
    tile = out.shape[1]

    def put(n, value):
        out[pl.ds(pl.multiple_of(slots[n] * tile, tile), tile), :] = value * scale

    put(0, r1[...].astype(f32))
    put(1, extra[...])
    put(2, r0[...].astype(f32))
    put(3, own[:, :tile].T)
    put(4, own[:, tile:].T)


def assemble(scale, slots, own, r0, r1, extra):
    tile = own.shape[0]
    return pl.pallas_call(
        functools.partial(assemble_body, scale),
        in_specs=[pl.BlockSpec(memory_space=pltpu.SMEM)] + [pl.BlockSpec(memory_space=pltpu.VMEM)] * 4,
        out_shape=jax.ShapeDtypeStruct((4 * tile, tile), f32),
        name="assemble",
    )(slots, own, r0, r1, extra)


def row_pair(t, c):
    u, m = t // 4, t % 4
    p = (t + (c > u)) % 2
    return jnp.where(c == u, m, p), jnp.where(c == u, (m + 1) % 4, p + 2)


def partner_moves(q):
    moves = []
    for t in range(NY * NZ * 2):
        for c in range(NC):
            u, m = t // 4, t % 4
            if c == u:
                r = (m + 1) % 4 if q == 0 else m
            else:
                r = (t + (c > u)) % 2 + 2 * ((q + m // 2) % 2)
            moves.append((t * NC + c, (4 * c + r) * NC + u))
    return moves


def shards(hidden, norm_gain, token_ids, owner, query_store, key_store):
    y, z, k = lax.axis_index("y"), lax.axis_index("zl"), lax.axis_index("k")
    column = lax.axis_index("x") * 2 + lax.axis_index("zh")
    root = owner[0]
    root_z, root_y, root_k = root // 8, (root // 2) % 4, root % 2

    tokens, depth = hidden.shape
    half = depth // 2
    piece = half // (NY * NZ)
    qwidth, kwidth = query_store.shape[2], key_store.shape[2]
    h = NZ // 2
    here = root_k == k

    q = query_store[0].reshape(2 * NY, 2, h * piece, qwidth)
    kt = key_store[0].T

    def stored(core, at):
        rows = pick(q, core * NY + at)
        start = (core * NY + at) * (NZ * piece)
        side = lax.dynamic_slice_in_dim(kt, start, NZ * piece, 1)
        side = jnp.stack([side[:, : h * piece], side[:, h * piece :]], axis=0)
        return jnp.concatenate([rows, side], axis=1)

    def block(rel, core, here):
        at = (y + rel) % NY
        return jnp.where(here, stored(core, at), send(stored(1 - core, at), "k", 1))

    step_y = (y - root_y) % NY
    far = block(2, k, here)
    far0, far1, later_k, later = together((far[0], far[1], k, here))
    a = send(far0, "y", 1)
    b = send(far1, "y", -1)
    up, down, own = (block(rel, later_k, later) for rel in (1, 3, 0))

    mine = normalize(hidden, norm_gain)
    mine, far0 = together((mine, far0))
    other = send(mine, "k", 1)

    up = jnp.where(step_y == 1, a[None], up)
    down = jnp.where(step_y == 3, b[None], down)
    up, down, other = together((up, down, other))
    c = send(up, "y", 1)
    d = send(down, "y", -1)

    zs = (z + jnp.arange(NZ)) % NZ
    rel = jnp.array([2, 1, 3, 0])[:, None]
    t = (zs[None] * (2 * NY) + ((y + rel) % NY) * 2 + k).reshape(-1)
    r0, r1 = row_pair(t, column)
    table = jnp.stack([t, 4 * column + r0, 4 * column + r1]).astype(jnp.int32)
    p_low, p_high, base = gram(table, mine, other)

    tile = depth // (NY * NZ * 2)
    both = [lax.dynamic_slice_in_dim(x, (4 * column + k) * tile, 3 * tile, 1) for x in (mine, other)]
    extra = sum(across(x[:, :tile], x[:, 2 * tile :]) for x in both)

    def butterfly(extra, axis, bit):
        pairs = [(i, i ^ bit) for i in range(SIZES[axis])]
        return lax.ppermute(extra.astype(bf16), axis, pairs).astype(f32)

    low = lax.broadcasted_iota(jnp.int32, (2, 1, 1), 0) == 0
    from_c = (step_y == 1) | ((step_y == 2) & low)
    quarter = jnp.where(step_y == 0, own, jnp.where(from_c, c, d))
    side = quarter[:, h * piece :].reshape(2, 2, kwidth // 2, 2, piece)
    side = side.transpose(0, 3, 2, 1, 4).reshape(NZ, kwidth // 2, 2 * piece)
    quarter = quarter[:, : h * piece].reshape(NZ, piece, qwidth)
    quarter = jnp.concatenate([quarter, side], axis=1)
    p_low, p_high, base, quarter, extra = together((p_low, p_high, base, quarter, extra))

    ga = send(p_low, "y", 1)
    gb = send(p_high, "y", -1)
    step_z = (z - root_z) % NZ
    got = [pick(quarter, z)] + [send(pick(quarter, (z + s) % NZ), "zl", s) for s in (1, 2, 3)]
    ea = butterfly(extra, "y", 1)
    first = lax.broadcasted_iota(jnp.int32, (2, 1, 1, 1), 0) == 0
    shape = (2, h, tile, 2 * tile)
    up = base[:NZ].reshape(shape) + jnp.where(first, ga.astype(f32)[None], 0.0)
    down = base[NZ : 2 * NZ].reshape(shape) + jnp.where(first, 0.0, gb.astype(f32)[None])
    up, down, step_z = together((up.astype(bf16), down.astype(bf16), step_z))
    gc = send(up, "y", 1).reshape(NZ, tile, 2 * tile)
    gd = send(down, "y", -1).reshape(NZ, tile, 2 * tile)
    extra = extra + ea
    eb = butterfly(extra, "y", 2)
    seed = got[0]
    for s in (1, 2, 3):
        seed = jnp.where(step_z == s, got[s], seed)
    strip = jnp.stack([seed] + [send(seed, "zl", -s) for s in (1, 2, 3)], axis=0)
    total = [base[2 * NZ + s] + gc[s].astype(f32) + gd[s].astype(f32) for s in range(NZ)]
    hess, rest = total[0], [x.astype(bf16) for x in total[1:]]
    extra = extra + eb
    strip, hess, rest, extra = together((strip, hess, rest, extra))

    def depth_tiles(rel):
        return (k * NY * NZ + ((y + rel) % NY) * NZ + zs).astype(jnp.int32)

    left = send(strip, "y", 1)
    right = send(strip, "y", -1)
    parts = [send(rest[s - 1], "zl", s) for s in (1, 2, 3)]
    ec = butterfly(extra, "zl", 1)
    raw = project(depth_tiles(0), mine, other, [strip])
    cosine, sine = turns(positions(token_ids))
    left, right, parts, ec, raw, cosine, sine = together((left, right, parts, ec, raw, cosine, sine))
    fl = send(left[:h], "y", 1)
    fr = send(right[h:], "y", -1)
    for part in parts:
        hess = hess + part.astype(f32)

    t = z * (2 * NY) + y * 2 + k
    u, m = t // 4, t % 4
    diagonal = column == u
    r0, r1 = row_pair(t, column)
    tiles, raw = together((hess.astype(bf16), raw))
    tiles = [tiles[:, :tile], tiles[:, tile:]]
    mirrored = []
    for n in (0, 1):
        second = jnp.where(diagonal, 1, (n + m // 2) % 2) == 1
        mirrored.append(lax.ppermute(jnp.where(second, tiles[1], tiles[0]), ALL, partner_moves(n)))
    extra = extra + ec
    extra = extra + butterfly(extra, "zl", 2)
    missing = 1 - r0 % 2
    slot0 = jnp.where(diagonal, (m + 3) % 4, missing + 2 * ((m // 2) % 2))
    slot1 = jnp.where(diagonal, (m + 2) % 4, missing + 2 * ((m // 2 + 1) % 2))
    slots = jnp.stack([slot1, jnp.where(diagonal, slot1, r0), slot0, r0, r1]).astype(jnp.int32)
    extra = jnp.where(m < 2, extra.T, extra)
    all_tokens = tokens * NY * NZ * 2
    hessian = assemble(2.0 / all_tokens, slots, hess, mirrored[0], mirrored[1], extra)

    tiles = jnp.concatenate([depth_tiles(3), depth_tiles(1)])
    raw = project(tiles, mine, other, [left, right], raw)
    raw = project(depth_tiles(2), mine, other, [fl, fr], raw)
    queries, keys = rope(raw, send(raw[1], "k", 1), cosine, sine)
    keys = lax.dynamic_slice_in_dim(keys, (column * kwidth) % HEAD, kwidth, 1)
    return (queries, keys, hessian)


def solution(mesh):
    fine = Mesh(mesh.devices.reshape(NZ, NY, 2, 4, 2), ALL)
    placed = (P(TOK, None), P(), P(TOK), P(), P(TOK, None, COL), P(TOK, None, COL))
    return jax.shard_map(
        shards,
        mesh=fine,
        in_specs=placed,
        out_specs=(P(TOK, COL), P(TOK, COL), P(COL, TOK)),
        check_vma=False,
    )
```

time: 515 us -> 235 us (0.46)
  waiting for transfers between devices: 337 us -> 95.8 us
  between operations: 15.2 us -> 1.88 us
  Pallas kernels: 49 us -> 36.1 us
  matrix products: 7.77 us -> 2.39 us
    psum x2 -> x0, waiting for transfers between devices: 281 us -> none  [the longest x1 161 us: shards(): extra = lax.psum(extra, ('zl', 'y'))]
    ppermute x2, waiting for transfers between devices: 0.01 us -> 24.8 us  [shards(): lax.ppermute(jnp.where(second, tiles[1], tiles[0]), ALL, partner_moves(n))]
    ppermute x0 -> x4, waiting for transfers between devices: none -> 18.3 us  [butterfly(): return lax.ppermute(extra.astype(bf16), axis, pairs).astype(f32)]
    pallas_call x10 -> x5, Pallas kernels: 46.6 us -> 33.7 us  [the longest x1 15.7 us: gram(): pl.pallas_call(gram_body, grid_spec=pltpu.PrefetchScalarGridSpec(num_scal...]
    select_n x7 -> x4, other arithmetic: 14 us -> 3.32 us  [the longest x1 1.47 us: shards(): up = jnp.where(step_y == 1, a[None], up)]
    convert_element_type x1 -> x10, other arithmetic: 2.25 us -> 11.2 us  [the longest x1 3.93 us: shards(): hess, rest = (total[0], [x.astype(bf16) for x in total[1:]])]
    ppermute x29 -> x27, starting transfers between devices: 38.1 us -> 30.7 us  [send(): return lax.ppermute(array, axis, [(i, (i + shift) % n) for i in range(n)])]
    ppermute x29 -> x27, waiting for transfers between devices: 56.1 us -> 52.7 us  [send(): return lax.ppermute(array, axis, [(i, (i + shift) % n) for i in range(n)])]
  transfers between devices with their start and end apart: 33 -> 33, of which waited for: 8 -> 13; matrix products, arithmetic and copies ran while one was open for 10% -> 17% of each run, Pallas kernels for 9% -> 14%
where the time goes in v2:
time: 235 us; the launch traced here: 233 us
  waiting for transfers between devices  95.8 us (41%)
  starting transfers between devices  45.6 us (19%)
  Pallas kernels  36.1 us (15%)
  other arithmetic  32.9 us (14%)
  local copies, waits for them, and re-layouts  18.7 us (8%)
  matrix products  2.39 us (1%)
    ppermute x27, waiting for transfers between devices, send(): return lax.ppermute(array, axis, [(i, (i + shift) % n) for i in range(n)])  52.7 us
    ppermute x27, starting transfers between devices, send(): return lax.ppermute(array, axis, [(i, (i + shift) % n) for i in range(n)])  30.7 us
    ppermute x2, waiting for transfers between devices, shards(): lax.ppermute(jnp.where(second, tiles[1], tiles[0]), ALL, partner_moves(n))  24.8 us
    ppermute x4, waiting for transfers between devices, butterfly(): return lax.ppermute(extra.astype(bf16), axis, pairs).astype(f32)  18.3 us
    pallas_call x1, Pallas kernels, gram(): pl.pallas_call(gram_body, grid_spec=pltpu.PrefetchScalarGridSpec(num_scal...  15.7 us
    pallas_call x3, Pallas kernels, project(): pl.pallas_call(functools.partial(project_body, slots, piece, fresh), grid...  15.6 us
    ppermute x2, starting transfers between devices, shards(): lax.ppermute(jnp.where(second, tiles[1], tiles[0]), ALL, partner_moves(n))  10.1 us
    squeeze x3, local copies, waits for them, and re-layouts, pick(): return lax.dynamic_index_in_dim(array, index, 0, keepdims=False)  5.72 us
  transfers between devices with their start and end apart: 33, of which 13 were waited for; matrix products, arithmetic and copies ran while one was open for 17% of the time, Pallas kernels for 14%

profile of v2, /device:TPU:132, one launch (start us, length us, event | category | flops | bytes accessed | tf_op | source)
XLA Modules:
  0.0 233.5 jit_solution(6576564709157172707)
XLA Ops:
  1.7 1.7 dynamic-slice_bitcast_fusion.7
  4.9 3.3 %fusion = f32[256]{0:T(256)S(1)} fusion(bf16[256,8192]{1,0:T(8,128)(2,1)} %param.7), kind=kLoop, calls=%fused_computation.2 | loop fusion | flops 6291200 | bytes 4195328 | tf_op jit(solution)/shard_map/reduce_sum | solution.py:57
  8.4 4.1 %fusion.2.refs_0_.refs_2_.refs_4_.refs_1_.refs_3_.refs_5_.refs_6_.refs_7_ = bf16[256,8192]{1,0:T(8,128)(2,1)} fusion(bf16[256,8192]{1,0:T(8,128)(2,1)S(1)} %copy-done, f32[8192]{0:T(1024)} %param.8, f32[256]{0:T(256)S(1)} %add_rsqrt_fusion), kind=kLoop, calls=%fused_computation.4 | loop fusion | flops 8388608 | bytes 8422400 | tf_op jit(solution)/shard_map/convert_element_type | solution.py:58
  14.1 3.2 %dynamic-slice_bitcast_fusion.1 = (bf16[2,512,512]{2,1,0:T(8,128)(2,1)S(1)}, bf16[2,512,512]{2,1,0:T(8,128)(2,1)S(1)}, bf16[2,512,512]{2,1,0:T(8,128)(2,1)S(1)},...) fusion(bf16[8,2,512,512]{3,2,1,0:T(8,128)(2,1)} %bitcast.134, ...), kind=kLoop, calls=%fused_computation.22 | loop fusion | bytes 12582936 | tf_op jit(solution)/shard_map/jit(dynamic_index_in_dim)/squeeze | solution.py:34
  18.9 1.6 collective-permute-start.1
  20.4 1.7 collective-permute-start.3
  23.2 12.7 %collective-permute-done.3 = bf16[576,512]{1,0:T(8,128)(2,1)S(1)} collective-permute-done((bf16[576,512]{1,0:T(8,128)(2,1)S(1)}, bf16[576,512]{1,0:T(8,128)(2,1)S(1)}, u32[]{:S(2)}, u32[]{:S(2)}) %collective-permute-start.3) | collective-permute-done | bytes 589856 | tf_op jit(solution)/shard_map/ppermute | solution.py:27
  35.9 1.5 fusion.4
  37.4 1.5 fusion.3
  38.8 1.6 collective-permute-start.7
  40.4 1.7 collective-permute-start.8
  42.1 1.2 fusion.17
  43.3 1.2 convolution_add_fusion
  44.5 15.7 %gram.1 = (bf16[2,256,512]{2,1,0:T(8,128)(2,1)}, bf16[2,256,512]{2,1,0:T(8,128)(2,1)}, f32[12,256,512]{2,1,0:T(8,128)}) custom-call(s32[3,16]{1,0:T(4,128)} %pad_add_fusion.table, bf16[256,8192]{1,0:T(8,128)(2,1)} %fusion.2.refs_0_.refs_2_.refs_4_.refs_1_.refs_3_.refs_5_.refs_6_.refs_7_, ...), custom_call_target="tpu_custom_call" | custom-call | flops 4294967296 | bytes 16777216 | tf_op jit(solution)/shard_map/gram/pallas_call | solution.py:95
  60.2 8.6 %collective-permute-done.7 = bf16[2,576,512]{2,1,0:T(8,128)(2,1)} collective-permute-done((bf16[2,576,512]{2,1,0:T(8,128)(2,1)}, bf16[2,576,512]{2,1,0:T(8,128)(2,1)}, u32[]{:S(2)}, u32[]{:S(2)}) %collective-permute-start.7) | collective-permute-done | bytes 1179680 | tf_op jit(solution)/shard_map/ppermute | solution.py:27
  68.8 2.4 %fusion.5 = bf16[2,576,512]{2,1,0:T(8,128)(2,1)S(1)} fusion(bf16[2,576,512]{2,1,0:T(8,128)(2,1)S(1)} %collective-permute-done.6, bf16[1,64,512]{2,1,0:T(8,128)(2,1)S(1)} %get-tuple-element.128, bf16[1,64,512]{2,1,0:T(8,128)(2,1)S(1)} %get-tuple-element.127, bf16[2,512,512]{2,1,0:T(8,128)(2,1)S(1)} %get-tuple-element.102, ...), kind=kLoop, calls=%fused_computation.16 | loop fusion | flops 5308416 | bytes 5898244 | tf_op jit(solution)/shard_map/jit(_where)/select_n | solution.py:297
  71.6 1.4 collective-permute-start.9
  73.0 2.0 collective-permute-start.10
  75.9 1.9 collective-permute-start.11
  78.4 2.7 %fusion.35 = (f32[4,256,512]{2,1,0:T(8,128)S(1)}, f32[4,256,512]{2,1,0:T(8,128)S(1)}) fusion(f32[12,256,512]{2,1,0:T(8,128)} %get-tuple-element.52), kind=kLoop, calls=%fused_computation.143 | loop fusion | bytes 8388608 | tf_op jit(solution)/shard_map/slice | solution.py:312
  81.1 5.5 %collective-permute-done.9 = bf16[2,256,512]{2,1,0:T(8,128)(2,1)S(1)} collective-permute-done((bf16[2,256,512]{2,1,0:T(8,128)(2,1)}, bf16[2,256,512]{2,1,0:T(8,128)(2,1)S(1)}, u32[]{:S(2)}, u32[]{:S(2)}) %collective-permute-start.9) | collective-permute-done | bytes 524320 | tf_op jit(solution)/shard_map/ppermute | solution.py:27
  87.9 1.9 add_convert_fusion
  89.8 1.2 collective-permute-start.17
  91.1 2.0 collective-permute-start.18
  94.3 1.6 collective-permute-start.20
  96.0 7.6 %collective-permute-done.12 = bf16[288,512]{1,0:T(8,128)(2,1)} collective-permute-done((bf16[288,512]{1,0:T(8,128)(2,1)S(1)}, bf16[288,512]{1,0:T(8,128)(2,1)}, u32[]{:S(2)}, u32[]{:S(2)}) %collective-permute-start.12) | collective-permute-done | bytes 294944 | tf_op jit(solution)/shard_map/ppermute | solution.py:27
  103.8 3.1 %collective-permute-start.15 = (bf16[288,512]{1,0:T(8,128)(2,1)S(1)}, bf16[288,512]{1,0:T(8,128)(2,1)S(1)}, u32[]{:S(2)}, u32[]{:S(2)}) collective-permute-start(bf16[288,512]{1,0:T(8,128)(2,1)S(1)} %fusion.7), channel_id=1, source_target_pairs={{0,128},{64,192},{128,0},{192,64},{1,129},{65,193},{129,1},{193,65... | collective-permute-start | bytes 884744 | tf_op jit(solution)/shard_map/ppermute | solution.py:27
  106.8 10.9 %collective-permute-done.20 = bf16[256,256]{1,0:T(8,128)(2,1)} collective-permute-done((bf16[256,256]{1,0:T(8,128)(2,1)}, bf16[256,256]{1,0:T(8,128)(2,1)}, u32[]{:S(2)}, u32[]{:S(2)}) %collective-permute-start.20) | collective-permute-done | bytes 131104 | tf_op jit(solution)/shard_map/ppermute | solution.py:293
  120.3 12.1 %collective-permute-done.15 = bf16[288,512]{1,0:T(8,128)(2,1)S(1)} collective-permute-done((bf16[288,512]{1,0:T(8,128)(2,1)S(1)}, bf16[288,512]{1,0:T(8,128)(2,1)S(1)}, u32[]{:S(2)}, u32[]{:S(2)}) %collective-permute-start.15) | collective-permute-done | bytes 294944 | tf_op jit(solution)/shard_map/ppermute | solution.py:27
  134.3 3.9 %fusion.10 = (bf16[256,512]{1,0:T(8,128)(2,1)}, bf16[256,512]{1,0:T(8,128)(2,1)}, bf16[256,512]{1,0:T(8,128)(2,1)}, f32[256,512]{1,0:T(8,128)}) fusion(f32[12,256,512]{2,1,0:T(8,128)} %get-tuple-element.52, bf16[4,256,512]{2,1,0:T(8,128)(2,1)} %bitcast.65, bf16[4,256,512]{2,1,0:T(8,128)(2,1)} %bitcast.64), kind=kLoop, calls=%fused_computation.45 | loop fusion | flops 2490368 | bytes 5505024 | tf_op jit(solution)/shard_map/convert_element_type | solution.py:323
  138.3 2.3 collective-permute-start.21
  144.1 2.0 collective-permute-start.23
  146.1 7.4 %collective-permute-done.26 = bf16[256,256]{1,0:T(8,128)(2,1)} collective-permute-done((bf16[256,256]{1,0:T(8,128)(2,1)}, bf16[256,256]{1,0:T(8,128)(2,1)}, u32[]{:S(2)}, u32[]{:S(2)}) %collective-permute-start.26) | collective-permute-done | bytes 131104 | tf_op jit(solution)/shard_map/ppermute | solution.py:293
  153.6 1.2 fusion.14
  154.8 4.4 %project.3.refs_18_ = f32[2,256,640]{2,1,0:T(8,128)} custom-call(s32[4]{0:T(128)} %broadcast_add_fusion.2.table, bf16[256,8192]{1,0:T(8,128)(2,1)} %fusion.2.refs_0_.refs_2_.refs_4_.refs_1_.refs_3_.refs_5_.refs_6_.refs_7_, bf16[256,8192]{1,0:T(8,128)(2,1)} %fusion.2.refs_0_.refs_2_.refs_4_.refs_1_.refs_3_.refs_5_.refs_6_.refs_7_, ...), custom_call_target="tpu_custom_call" | custom-call | flops 536870912 | bytes 4325376 | tf_op jit(solution)/shard_map/project/pallas_call | solution.py:149
  160.2 4.0 %collective-permute-done.24 = bf16[256,512]{1,0:T(8,128)(2,1)} collective-permute-done((bf16[256,512]{1,0:T(8,128)(2,1)}, bf16[256,512]{1,0:T(8,128)(2,1)}, u32[]{:S(2)}, u32[]{:S(2)}) %collective-permute-start.24) | collective-permute-done | bytes 262176 | tf_op jit(solution)/shard_map/ppermute | solution.py:27
  165.1 1.2 collective-permute-done.21.refs_16_
  168.1 3.2 %collective-permute-start.28 = (bf16[2,288,512]{2,1,0:T(8,128)(2,1)}, bf16[2,288,512]{2,1,0:T(8,128)(2,1)}, u32[]{:S(2)}, u32[]{:S(2)}) collective-permute-start(bf16[2,288,512]{2,1,0:T(8,128)(2,1)} %slice.168), channel_id=1, source_target_pairs={{0,48},{16,0},{32,16},{48,32},{1,49},{17,1},{33,17},{49,33},{2,50}... | collective-permute-start | bytes 1769480 | tf_op jit(solution)/shard_map/ppermute | solution.py:27
  172.1 3.0 %collective-permute-start.32 = (bf16[256,256]{1,0:T(8,128)(2,1)}, bf16[256,256]{1,0:T(8,128)(2,1)S(1)}, u32[]{:S(2)}, u32[]{:S(2)}) collective-permute-start(bf16[256,256]{1,0:T(8,128)(2,1)} %get-tuple-element.91), channel_id=1, source_target_pairs={{0,128},{64,192},{128,0},{192,64},{1,129},{65,193},{129,1},{193,65... | collective-permute-start | bytes 393224 | tf_op jit(solution)/shard_map/ppermute | solution.py:293
  175.1 2.0 fusion.34
  177.2 6.3 %project.4.refs_10_ = f32[2,256,640]{2,1,0:T(8,128)} custom-call(s32[8]{0:T(128)} %pad_add_fusion.1.table, bf16[256,8192]{1,0:T(8,128)(2,1)} %fusion.2.refs_0_.refs_2_.refs_4_.refs_1_.refs_3_.refs_5_.refs_6_.refs_7_, bf16[256,8192]{1,0:T(8,128)(2,1)} %fusion.2.refs_0_.refs_2_.refs_4_.refs_1_.refs_3_.refs_5_.refs_6_.refs_7_, ...), custom_call_target="tpu_custom_call" | custom-call | flops 1073741824 | bytes 6553600 | tf_op jit(solution)/shard_map/project/pallas_call | solution.py:149
  183.5 4.9 %project.5.a = f32[2,256,640]{2,1,0:T(8,128)} custom-call(s32[4]{0:T(128)} %broadcast_add_fusion.3.table, bf16[256,8192]{1,0:T(8,128)(2,1)} %fusion.2.refs_0_.refs_2_.refs_4_.refs_1_.refs_3_.refs_5_.refs_6_.refs_7_, bf16[256,8192]{1,0:T(8,128)(2,1)} %fusion.2.refs_0_.refs_2_.refs_4_.refs_1_.refs_3_.refs_5_.refs_6_.refs_7_, ...), custom_call_target="tpu_custom_call" | custom-call | flops 536870912 | bytes 4325376 | tf_op jit(solution)/shard_map/project/pallas_call | solution.py:149
  188.4 1.1 slice_bitcast_fusion
  189.7 10.0 %collective-permute-start.31 = (bf16[256,256]{1,0:T(8,128)(2,1)S(1)}, bf16[256,256]{1,0:T(8,128)(2,1)S(1)}, u32[]{:S(2)}, u32[]{:S(2)}) collective-permute-start(bf16[256,256]{1,0:T(8,128)(2,1)S(1)} %get-tuple-element.125), channel_id=1, source_target_pairs={{0,0},{1,56},{2,88},{3,120},{4,152},{5,184},{6,216},{7,248},{8,8},... | collective-permute-start | bytes 393224 | tf_op jit(solution)/shard_map/ppermute | solution.py:351
  200.7 18.4 %collective-permute-done.30.r0 = bf16[256,256]{1,0:T(8,128)(2,1)S(1)} collective-permute-done((bf16[256,256]{1,0:T(8,128)(2,1)S(1)}, bf16[256,256]{1,0:T(8,128)(2,1)S(1)}, u32[]{:S(2)}, u32[]{:S(2)}) %collective-permute-start.30) | collective-permute-done | bytes 131104 | tf_op jit(solution)/shard_map/ppermute | solution.py:351
  219.1 6.4 %collective-permute-done.31.r1 = bf16[256,256]{1,0:T(8,128)(2,1)S(1)} collective-permute-done((bf16[256,256]{1,0:T(8,128)(2,1)S(1)}, bf16[256,256]{1,0:T(8,128)(2,1)S(1)}, u32[]{:S(2)}, u32[]{:S(2)}) %collective-permute-start.31) | collective-permute-done | bytes 131104 | tf_op jit(solution)/shard_map/ppermute | solution.py:351
  226.2 2.4 %assemble.1 = f32[1024,256]{1,0:T(8,128)} custom-call(s32[5]{0:T(128)} %stack.145.slots, f32[256,512]{1,0:T(8,128)} %get-tuple-element.94.own, bf16[256,256]{1,0:T(8,128)(2,1)} %copy-done.12, bf16[256,256]{1,0:T(8,128)(2,1)} %copy-done.13, f32[256,256]{1,0:T(8,128)} %fusion.12.extra), custom_call_target="tpu_custom_call" | custom-call | tf_op jit(solution)/shard_map/assemble/pallas_call | solution.py:209
  229.4 2.4 %rope.1 = (bf16[256,512]{1,0:T(8,128)(2,1)}, bf16[256,128]{1,0:T(8,128)(2,1)}) custom-call(f32[2,256,640]{2,1,0:T(8,128)} %project.5.a, f32[256,640]{1,0:T(8,128)} %copy-done.8, f32[256,128]{1,0:T(8,128)} %get-tuple-element.73.cosine, f32[256,128]{1,0:T(8,128)} %get-tuple-element.74.sine), custom_call_target="tpu_custom_call" | custom-call | tf_op jit(solution)/shard_map/rope/pallas_call | solution.py:184
  (134 shorter events, 27.4 us)
Async XLA Ops:
  3.5 8.9 %collective-permute-start = (bf16[2,576,512]{2,1,0:T(8,128)(2,1)S(1)}, bf16[2,576,512]{2,1,0:T(8,128)(2,1)S(1)}, u32[]{:S(2)}, u32[]{:S(2)}) collective-permute-start(bf16[2,576,512]{2,1,0:T(8,128)(2,1)S(1)} %maximum_maximum_fusion), channel_id=1, source_target_pairs={{0,8},{8,0},{1,9},{9,1},{2,10},{10,2},{3,11},{11,3},{4,12},{12,4},... | collective-permute-start | bytes 3538952 | tf_op jit(solution)/shard_map/ppermute | solution.py:27
  4.9 3.4 %copy-start = (bf16[256,8192]{1,0:T(8,128)(2,1)S(1)}, bf16[256,8192]{1,0:T(8,128)(2,1)}, u32[]{:S(2)}) copy-start(bf16[256,8192]{1,0:T(8,128)(2,1)} %param.7) | copy-start | bytes 12582916
  8.4 4.1 %copy-start.10 = (bf16[1,64,512]{2,1,0:T(8,128)(2,1)S(1)}, bf16[1,64,512]{2,1,0:T(8,128)(2,1)}, u32[]{:S(2)}) copy-start(bf16[1,64,512]{2,1,0:T(8,128)(2,1)} %get-tuple-element.139) | copy-start | bytes 196612
  8.4 4.1 %copy-start.11 = (bf16[1,64,512]{2,1,0:T(8,128)(2,1)S(1)}, bf16[1,64,512]{2,1,0:T(8,128)(2,1)}, u32[]{:S(2)}) copy-start(bf16[1,64,512]{2,1,0:T(8,128)(2,1)} %get-tuple-element.140) | copy-start | bytes 196612
  12.8 1.2 copy-start.7
  12.9 25.9 %collective-permute-start.5 = (bf16[256,8192]{1,0:T(8,128)(2,1)}, bf16[256,8192]{1,0:T(8,128)(2,1)}, u32[]{:S(2)}, u32[]{:S(2)}) collective-permute-start(bf16[256,8192]{1,0:T(8,128)(2,1)} %fusion.2.refs_0_.refs_2_.refs_4_.refs_1_.refs_3_.refs_5_.refs_6_.refs_7_), channel_id=1, source_target_pairs={{0,8},{8,0},{1,9},{9,1},{2,10},{10,2},{3,11},{11,3},{4,12},{12,4},... | collective-permute-start | bytes 12582920 | tf_op jit(solution)/shard_map/ppermute | solution.py:27
  17.5 18.4 %collective-permute-start.4 = (bf16[2,576,512]{2,1,0:T(8,128)(2,1)S(1)}, bf16[2,576,512]{2,1,0:T(8,128)(2,1)S(1)}, u32[]{:S(2)}, u32[]{:S(2)}) collective-permute-start(bf16[2,576,512]{2,1,0:T(8,128)(2,1)S(1)} %maximum_maximum_fusion.2), channel_id=1, source_target_pairs={{0,8},{8,0},{1,9},{9,1},{2,10},{10,2},{3,11},{11,3},{4,12},{12,4},... | collective-permute-start | bytes 3538952 | tf_op jit(solution)/shard_map/ppermute | solution.py:27
  18.1 19.2 %collective-permute-start.2 = (bf16[2,576,512]{2,1,0:T(8,128)(2,1)S(1)}, bf16[2,576,512]{2,1,0:T(8,128)(2,1)S(1)}, u32[]{:S(2)}, u32[]{:S(2)}) collective-permute-start(bf16[2,576,512]{2,1,0:T(8,128)(2,1)S(1)} %maximum_maximum_fusion.1), channel_id=1, source_target_pairs={{0,8},{8,0},{1,9},{9,1},{2,10},{10,2},{3,11},{11,3},{4,12},{12,4},... | collective-permute-start | bytes 3538952 | tf_op jit(solution)/shard_map/ppermute | solution.py:27
  18.9 18.5 %collective-permute-start.1 = (bf16[576,512]{1,0:T(8,128)(2,1)S(1)}, bf16[576,512]{1,0:T(8,128)(2,1)S(1)}, u32[]{:S(2)}, u32[]{:S(2)}) collective-permute-start(bf16[576,512]{1,0:T(8,128)(2,1)S(1)} %get-tuple-element.41), channel_id=1, source_target_pairs={{0,16},{16,32},{32,48},{48,0},{1,17},{17,33},{33,49},{49,1},{2,18}... | collective-permute-start | bytes 1769480 | tf_op jit(solution)/shard_map/ppermute | solution.py:27
  20.4 15.4 %collective-permute-start.3 = (bf16[576,512]{1,0:T(8,128)(2,1)S(1)}, bf16[576,512]{1,0:T(8,128)(2,1)S(1)}, u32[]{:S(2)}, u32[]{:S(2)}) collective-permute-start(bf16[576,512]{1,0:T(8,128)(2,1)S(1)} %get-tuple-element.45), channel_id=1, source_target_pairs={{0,48},{16,0},{32,16},{48,32},{1,49},{17,1},{33,17},{49,33},{2,50}... | collective-permute-start | bytes 1769480 | tf_op jit(solution)/shard_map/ppermute | solution.py:27
  35.9 24.3 %collective-permute-start.6 = (bf16[2,576,512]{2,1,0:T(8,128)(2,1)}, bf16[2,576,512]{2,1,0:T(8,128)(2,1)S(1)}, u32[]{:S(2)}, u32[]{:S(2)}) collective-permute-start(bf16[2,576,512]{2,1,0:T(8,128)(2,1)} %maximum_maximum_fusion.3), channel_id=1, source_target_pairs={{0,8},{8,0},{1,9},{9,1},{2,10},{10,2},{3,11},{11,3},{4,12},{12,4},... | collective-permute-start | bytes 3538952 | tf_op jit(solution)/shard_map/ppermute | solution.py:27
  38.8 29.9 %collective-permute-start.7 = (bf16[2,576,512]{2,1,0:T(8,128)(2,1)}, bf16[2,576,512]{2,1,0:T(8,128)(2,1)}, u32[]{:S(2)}, u32[]{:S(2)}) collective-permute-start(bf16[2,576,512]{2,1,0:T(8,128)(2,1)} %fusion.3), channel_id=1, source_target_pairs={{0,16},{16,32},{32,48},{48,0},{1,17},{17,33},{33,49},{49,1},{2,18}... | collective-permute-start | bytes 3538952 | tf_op jit(solution)/shard_map/ppermute | solution.py:27
  40.4 28.4 %collective-permute-start.8 = (bf16[2,576,512]{2,1,0:T(8,128)(2,1)}, bf16[2,576,512]{2,1,0:T(8,128)(2,1)}, u32[]{:S(2)}, u32[]{:S(2)}) collective-permute-start(bf16[2,576,512]{2,1,0:T(8,128)(2,1)} %fusion.4), channel_id=1, source_target_pairs={{0,48},{16,0},{32,16},{48,32},{1,49},{17,1},{33,17},{49,33},{2,50}... | collective-permute-start | bytes 3538952 | tf_op jit(solution)/shard_map/ppermute | solution.py:27
  71.6 15.0 %collective-permute-start.9 = (bf16[2,256,512]{2,1,0:T(8,128)(2,1)}, bf16[2,256,512]{2,1,0:T(8,128)(2,1)S(1)}, u32[]{:S(2)}, u32[]{:S(2)}) collective-permute-start(bf16[2,256,512]{2,1,0:T(8,128)(2,1)} %get-tuple-element.53), channel_id=1, source_target_pairs={{0,16},{16,32},{32,48},{48,0},{1,17},{17,33},{33,49},{49,1},{2,18}... | collective-permute-start | bytes 1572872 | tf_op jit(solution)/shard_map/ppermute | solution.py:27
  73.0 14.8 %collective-permute-start.10 = (bf16[2,256,512]{2,1,0:T(8,128)(2,1)}, bf16[2,256,512]{2,1,0:T(8,128)(2,1)S(1)}, u32[]{:S(2)}, u32[]{:S(2)}) collective-permute-start(bf16[2,256,512]{2,1,0:T(8,128)(2,1)} %get-tuple-element.54), channel_id=1, source_target_pairs={{0,48},{16,0},{32,16},{48,32},{1,49},{17,1},{33,17},{49,33},{2,50}... | collective-permute-start | bytes 1572872 | tf_op jit(solution)/shard_map/ppermute | solution.py:27
  75.0 16.1 %collective-permute-start.19 = (bf16[256,256]{1,0:T(8,128)(2,1)S(1)}, bf16[256,256]{1,0:T(8,128)(2,1)S(1)}, u32[]{:S(2)}, u32[]{:S(2)}) collective-permute-start(bf16[256,256]{1,0:T(8,128)(2,1)S(1)} %convert_element_type.159), channel_id=1, source_target_pairs={{0,16},{16,0},{32,48},{48,32},{1,17},{17,1},{33,49},{49,33},{2,18}... | collective-permute-start | bytes 393224 | tf_op jit(solution)/shard_map/ppermute | solution.py:293
  75.9 18.4 %collective-permute-start.11 = (bf16[288,512]{1,0:T(8,128)(2,1)}, bf16[288,512]{1,0:T(8,128)(2,1)}, u32[]{:S(2)}, u32[]{:S(2)}) collective-permute-start(bf16[288,512]{1,0:T(8,128)(2,1)} %get-tuple-element.114), channel_id=1, source_target_pairs={{0,192},{64,0},{128,64},{192,128},{1,193},{65,1},{129,65},{193,129... | collective-permute-start | bytes 884744 | tf_op jit(solution)/shard_map/ppermute | solution.py:27
  77.8 25.8 %collective-permute-start.12 = (bf16[288,512]{1,0:T(8,128)(2,1)S(1)}, bf16[288,512]{1,0:T(8,128)(2,1)}, u32[]{:S(2)}, u32[]{:S(2)}) collective-permute-start(bf16[288,512]{1,0:T(8,128)(2,1)S(1)} %get-tuple-element.113), channel_id=1, source_target_pairs={{0,128},{64,192},{128,0},{192,64},{1,129},{65,193},{129,1},{193,65... | collective-permute-start | bytes 884744 | tf_op jit(solution)/shard_map/ppermute | solution.py:27
  86.6 17.0 %collective-permute-start.13 = (bf16[288,512]{1,0:T(8,128)(2,1)S(1)}, bf16[288,512]{1,0:T(8,128)(2,1)}, u32[]{:S(2)}, u32[]{:S(2)}) collective-permute-start(bf16[288,512]{1,0:T(8,128)(2,1)S(1)} %get-tuple-element.112), channel_id=1, source_target_pairs={{0,64},{64,128},{128,192},{192,0},{1,65},{65,129},{129,193},{193,1... | collective-permute-start | bytes 884744 | tf_op jit(solution)/shard_map/ppermute | solution.py:27
  89.8 44.5 %collective-permute-start.17 = (bf16[2,2,256,512]{3,2,1,0:T(8,128)(2,1)}, bf16[2,2,256,512]{3,2,1,0:T(8,128)(2,1)}, u32[]{:S(2)}, u32[]{:S(2)}) collective-permute-start(bf16[2,2,256,512]{3,2,1,0:T(8,128)(2,1)} %get-tuple-element.57), channel_id=1, source_target_pairs={{0,16},{16,32},{32,48},{48,0},{1,17},{17,33},{33,49},{49,1},{2,18}... | collective-permute-start | bytes 3145736 | tf_op jit(solution)/shard_map/ppermute | solution.py:27
  91.1 43.2 %collective-permute-start.18 = (bf16[2,2,256,512]{3,2,1,0:T(8,128)(2,1)S(1)}, bf16[2,2,256,512]{3,2,1,0:T(8,128)(2,1)}, u32[]{:S(2)}, u32[]{:S(2)}) collective-permute-start(bf16[2,2,256,512]{3,2,1,0:T(8,128)(2,1)S(1)} %get-tuple-element.58), channel_id=1, source_target_pairs={{0,48},{16,0},{32,16},{48,32},{1,49},{17,1},{33,17},{49,33},{2,50}... | collective-permute-start | bytes 3145736 | tf_op jit(solution)/shard_map/ppermute | solution.py:27
  94.3 23.4 %collective-permute-start.20 = (bf16[256,256]{1,0:T(8,128)(2,1)}, bf16[256,256]{1,0:T(8,128)(2,1)}, u32[]{:S(2)}, u32[]{:S(2)}) collective-permute-start(bf16[256,256]{1,0:T(8,128)(2,1)} %fusion.11), channel_id=1, source_target_pairs={{0,32},{16,48},{32,0},{48,16},{1,33},{17,49},{33,1},{49,17},{2,34}... | collective-permute-start | bytes 393224 | tf_op jit(solution)/shard_map/ppermute | solution.py:293
  103.7 16.6 %collective-permute-start.14 = (bf16[288,512]{1,0:T(8,128)(2,1)S(1)}, bf16[288,512]{1,0:T(8,128)(2,1)S(1)}, u32[]{:S(2)}, u32[]{:S(2)}) collective-permute-start(bf16[288,512]{1,0:T(8,128)(2,1)S(1)} %fusion.7), channel_id=1, source_target_pairs={{0,192},{64,0},{128,64},{192,128},{1,193},{65,1},{129,65},{193,129... | collective-permute-start | bytes 884744 | tf_op jit(solution)/shard_map/ppermute | solution.py:27
  103.8 28.7 %collective-permute-start.15 = (bf16[288,512]{1,0:T(8,128)(2,1)S(1)}, bf16[288,512]{1,0:T(8,128)(2,1)S(1)}, u32[]{:S(2)}, u32[]{:S(2)}) collective-permute-start(bf16[288,512]{1,0:T(8,128)(2,1)S(1)} %fusion.7), channel_id=1, source_target_pairs={{0,128},{64,192},{128,0},{192,64},{1,129},{65,193},{129,1},{193,65... | collective-permute-start | bytes 884744 | tf_op jit(solution)/shard_map/ppermute | solution.py:27
  117.7 14.7 %collective-permute-start.16 = (bf16[288,512]{1,0:T(8,128)(2,1)S(1)}, bf16[288,512]{1,0:T(8,128)(2,1)S(1)}, u32[]{:S(2)}, u32[]{:S(2)}) collective-permute-start(bf16[288,512]{1,0:T(8,128)(2,1)S(1)} %fusion.7), channel_id=1, source_target_pairs={{0,64},{64,128},{128,192},{192,0},{1,65},{65,129},{129,193},{193,1... | collective-permute-start | bytes 884744 | tf_op jit(solution)/shard_map/ppermute | solution.py:27
  120.3 21.9 %copy-start.4 = (f32[256,256]{1,0:T(8,128)}, f32[256,256]{1,0:T(8,128)S(1)}, u32[]{:S(2)}) copy-start(f32[256,256]{1,0:T(8,128)S(1)} %convert_add_fusion.2) | copy-start | bytes 786436
  134.3 6.3 %copy-start.1 = (bf16[4,288,512]{2,1,0:T(8,128)(2,1)}, bf16[4,288,512]{2,1,0:T(8,128)(2,1)S(1)}, u32[]{:S(2)}) copy-start(bf16[4,288,512]{2,1,0:T(8,128)(2,1)S(1)} %pad_maximum_fusion.1.refs_8_) | copy-start | bytes 3538948
  134.3 7.7 %copy-start.14 = (s32[256]{0:T(256)S(1)}, s32[256]{0:T(256)}, u32[]{:S(2)}) copy-start(s32[256]{0:T(256)} %param.9) | copy-start | bytes 3076
  134.3 8.5 %copy-start.16 = (s32[4]{0:T(128)S(1)}, s32[4]{0:T(128)}, u32[]{:S(2)}) copy-start(s32[4]{0:T(128)} %get-tuple-element.151) | copy-start | bytes 52
  134.3 8.5 %copy-start.17 = (s32[4]{0:T(128)S(1)}, s32[4]{0:T(128)}, u32[]{:S(2)}) copy-start(s32[4]{0:T(128)} %get-tuple-element.152) | copy-start | bytes 52
  138.3 28.1 %collective-permute-start.21 = (bf16[4,288,512]{2,1,0:T(8,128)(2,1)S(1)}, bf16[4,288,512]{2,1,0:T(8,128)(2,1)S(1)}, u32[]{:S(2)}, u32[]{:S(2)}) collective-permute-start(bf16[4,288,512]{2,1,0:T(8,128)(2,1)S(1)} %pad_maximum_fusion.1.refs_8_), channel_id=1, source_target_pairs={{0,16},{16,32},{32,48},{48,0},{1,17},{17,33},{33,49},{49,1},{2,18}... | collective-permute-start | bytes 3538952 | tf_op jit(solution)/shard_map/ppermute | solution.py:27
  140.6 25.7 %collective-permute-start.22 = (bf16[4,288,512]{2,1,0:T(8,128)(2,1)S(1)}, bf16[4,288,512]{2,1,0:T(8,128)(2,1)S(1)}, u32[]{:S(2)}, u32[]{:S(2)}) collective-permute-start(bf16[4,288,512]{2,1,0:T(8,128)(2,1)S(1)} %pad_maximum_fusion.1.refs_8_), channel_id=1, source_target_pairs={{0,48},{16,0},{32,16},{48,32},{1,49},{17,1},{33,17},{49,33},{2,50}... | collective-permute-start | bytes 3538952 | tf_op jit(solution)/shard_map/ppermute | solution.py:27
  142.8 10.7 %collective-permute-start.26 = (bf16[256,256]{1,0:T(8,128)(2,1)}, bf16[256,256]{1,0:T(8,128)(2,1)}, u32[]{:S(2)}, u32[]{:S(2)}) collective-permute-start(bf16[256,256]{1,0:T(8,128)(2,1)} %convert_element_type.163), channel_id=1, source_target_pairs={{0,64},{64,0},{128,192},{192,128},{1,65},{65,1},{129,193},{193,129... | collective-permute-start | bytes 393224 | tf_op jit(solution)/shard_map/ppermute | solution.py:293
  144.1 16.1 %collective-permute-start.23 = (bf16[256,512]{1,0:T(8,128)(2,1)}, bf16[256,512]{1,0:T(8,128)(2,1)}, u32[]{:S(2)}, u32[]{:S(2)}) collective-permute-start(bf16[256,512]{1,0:T(8,128)(2,1)} %get-tuple-element.61), channel_id=1, source_target_pairs={{0,64},{64,128},{128,192},{192,0},{1,65},{65,129},{129,193},{193,1... | collective-permute-start | bytes 786440 | tf_op jit(solution)/shard_map/ppermute | solution.py:27
  146.1 18.1 %collective-permute-start.24 = (bf16[256,512]{1,0:T(8,128)(2,1)}, bf16[256,512]{1,0:T(8,128)(2,1)}, u32[]{:S(2)}, u32[]{:S(2)}) collective-permute-start(bf16[256,512]{1,0:T(8,128)(2,1)} %get-tuple-element.62), channel_id=1, source_target_pairs={{0,128},{64,192},{128,0},{192,64},{1,129},{65,193},{129,1},{193,65... | collective-permute-start | bytes 786440 | tf_op jit(solution)/shard_map/ppermute | solution.py:27
  153.6 11.6 %collective-permute-start.25 = (bf16[256,512]{1,0:T(8,128)(2,1)}, bf16[256,512]{1,0:T(8,128)(2,1)}, u32[]{:S(2)}, u32[]{:S(2)}) collective-permute-start(bf16[256,512]{1,0:T(8,128)(2,1)} %get-tuple-element.63), channel_id=1, source_target_pairs={{0,192},{64,0},{128,64},{192,128},{1,193},{65,1},{129,65},{193,129... | collective-permute-start | bytes 786440 | tf_op jit(solution)/shard_map/ppermute | solution.py:27
  159.3 12.1 %copy-start.5 = (f32[256,256]{1,0:T(8,128)S(1)}, f32[256,256]{1,0:T(8,128)}, u32[]{:S(2)}) copy-start(f32[256,256]{1,0:T(8,128)} %copy-done.4) | copy-start | bytes 786436
  166.3 5.8 %copy-start.2 = (bf16[4,288,512]{2,1,0:T(8,128)(2,1)}, bf16[4,288,512]{2,1,0:T(8,128)(2,1)S(1)}, u32[]{:S(2)}) copy-start(bf16[4,288,512]{2,1,0:T(8,128)(2,1)S(1)} %collective-permute-done.21.refs_16_) | copy-start | bytes 3538948
  166.3 5.7 %copy-start.3 = (bf16[4,288,512]{2,1,0:T(8,128)(2,1)}, bf16[4,288,512]{2,1,0:T(8,128)(2,1)S(1)}, u32[]{:S(2)}) copy-start(bf16[4,288,512]{2,1,0:T(8,128)(2,1)S(1)} %collective-permute-done.22.refs_17_) | copy-start | bytes 3538948
  167.2 7.9 %copy-start.6 = (f32[256,512]{1,0:T(8,128)S(1)}, f32[256,512]{1,0:T(8,128)}, u32[]{:S(2)}) copy-start(f32[256,512]{1,0:T(8,128)} %get-tuple-element.67) | copy-start | bytes 1572868
  167.2 16.2 %collective-permute-start.27 = (bf16[2,288,512]{2,1,0:T(8,128)(2,1)}, bf16[2,288,512]{2,1,0:T(8,128)(2,1)}, u32[]{:S(2)}, u32[]{:S(2)}) collective-permute-start(bf16[2,288,512]{2,1,0:T(8,128)(2,1)} %slice.167), channel_id=1, source_target_pairs={{0,16},{16,32},{32,48},{48,0},{1,17},{17,33},{33,49},{49,1},{2,18}... | collective-permute-start | bytes 1769480 | tf_op jit(solution)/shard_map/ppermute | solution.py:27
  168.1 15.4 %collective-permute-start.28 = (bf16[2,288,512]{2,1,0:T(8,128)(2,1)}, bf16[2,288,512]{2,1,0:T(8,128)(2,1)}, u32[]{:S(2)}, u32[]{:S(2)}) collective-permute-start(bf16[2,288,512]{2,1,0:T(8,128)(2,1)} %slice.168), channel_id=1, source_target_pairs={{0,48},{16,0},{32,16},{48,32},{1,49},{17,1},{33,17},{49,33},{2,50}... | collective-permute-start | bytes 1769480 | tf_op jit(solution)/shard_map/ppermute | solution.py:27
  172.1 27.7 %collective-permute-start.32 = (bf16[256,256]{1,0:T(8,128)(2,1)}, bf16[256,256]{1,0:T(8,128)(2,1)S(1)}, u32[]{:S(2)}, u32[]{:S(2)}) collective-permute-start(bf16[256,256]{1,0:T(8,128)(2,1)} %get-tuple-element.91), channel_id=1, source_target_pairs={{0,128},{64,192},{128,0},{192,64},{1,129},{65,193},{129,1},{193,65... | collective-permute-start | bytes 393224 | tf_op jit(solution)/shard_map/ppermute | solution.py:293
  189.5 39.1 %collective-permute-start.29 = (f32[256,640]{1,0:T(8,128)S(1)}, f32[256,640]{1,0:T(8,128)S(1)}, u32[]{:S(2)}, u32[]{:S(2)}) collective-permute-start(f32[256,640]{1,0:T(8,128)S(1)} %slice_bitcast_fusion), channel_id=1, source_target_pairs={{0,8},{8,0},{1,9},{9,1},{2,10},{10,2},{3,11},{11,3},{4,12},{12,4},... | collective-permute-start | bytes 1966088 | tf_op jit(solution)/shard_map/ppermute | solution.py:27
  189.6 29.5 %collective-permute-start.30 = (bf16[256,256]{1,0:T(8,128)(2,1)S(1)}, bf16[256,256]{1,0:T(8,128)(2,1)S(1)}, u32[]{:S(2)}, u32[]{:S(2)}) collective-permute-start(bf16[256,256]{1,0:T(8,128)(2,1)S(1)} %get-tuple-element.126), channel_id=1, source_target_pairs={{0,8},{1,40},{2,72},{3,104},{4,136},{5,168},{6,200},{7,232},{8,16}... | collective-permute-start | bytes 393224 | tf_op jit(solution)/shard_map/ppermute | solution.py:351
  189.7 35.8 %collective-permute-start.31 = (bf16[256,256]{1,0:T(8,128)(2,1)S(1)}, bf16[256,256]{1,0:T(8,128)(2,1)S(1)}, u32[]{:S(2)}, u32[]{:S(2)}) collective-permute-start(bf16[256,256]{1,0:T(8,128)(2,1)S(1)} %get-tuple-element.125), channel_id=1, source_target_pairs={{0,0},{1,56},{2,88},{3,120},{4,152},{5,184},{6,216},{7,248},{8,8},... | collective-permute-start | bytes 393224 | tf_op jit(solution)/shard_map/ppermute | solution.py:351
  219.1 6.4 %copy-start.12 = (bf16[256,256]{1,0:T(8,128)(2,1)}, bf16[256,256]{1,0:T(8,128)(2,1)S(1)}, u32[]{:S(2)}) copy-start(bf16[256,256]{1,0:T(8,128)(2,1)S(1)} %collective-permute-done.30.r0) | copy-start | bytes 393220
  228.6 0.9 copy-start.8
  (3 other events, 2.1 us)
